TPU v7x, 768 devices: a whole 4x8x12 slice. The times are simulated.
768 devices in a mesh: pos: 96 (over y, z), col: 8 (over x, core).
Axes of the slice: x: 4, y: 8, z: 12, core: 2. Of those that a mesh axis runs over, the one named last changes fastest.
Arguments:
- object_layers: float32 [2, 2, 768, 768], P(None, None, 'pos', 'col'), may hold values from -6 to 6
- probe_field: float32 [2, 256, 256], P(None, 'col'), may hold values from -6 to 6
- prop_phase: float32 [256, 256], P(None, 'col'), may hold values from -3.140625 to 3.140625
- amplitude: float32 [96, 256, 256], P('pos', None, 'col'), may hold values from 0 to 2
- offsets: int32 [96, 2], P('pos'), may hold values from 0 to 512
- counts: int32 [96], P('pos'), may hold values from 1 to 1, as said below
Outputs:
- object_grad: float32 [2, 2, 768, 768], P(None, None, 'pos', 'col')
Inputs may be any that keep to these rules, and one draw needn't show every extreme that they name: `counts`: slots of a pos index at or above its count are padding; some index of pos is full in every draw.
All inputs are finite; a program needn't handle non-finite values.
Results may differ from a plain program's by a relative error of at most 0.0003.
Values sent between devices are 32-bit elements; how exact they have to be, the bound alone decides.
No kernel may reach another device: no remote copies, remote signals or barrier semaphores. Data moves between devices by JAX's collectives and lax.ppermute only.
A program may use at most 32 MiB of HBM per device.

v0:
```python
import jax
import jax.numpy as jnp
from jax import lax
from jax.sharding import Mesh
from jax.sharding import PartitionSpec as P

POS = ("pos_0", "pos_1")


MOD_FLOOR = 0.1
EXACT_MODE = lax.Precision.HIGHEST


def in_one_piece(arrays, axis, split_dim, concat_dim, along):
    widths = [a.shape[along] for a in arrays]
    both = jnp.concatenate(arrays, axis=along)
    result = lax.all_to_all(both, axis, split_axis=split_dim, concat_axis=concat_dim, tiled=True)
    return tuple(jnp.split(result, [sum(widths[:k]) for k in range(1, len(widths))], axis=along))


def in_order(tiles, dim):
    tiles = jnp.moveaxis(tiles, 0, dim)
    shape = tiles.shape
    return tiles.reshape(*shape[:dim], shape[dim] * shape[dim + 1], *shape[dim + 2 :])


def gather_in_order(x, axes, sequence):
    tiles = x[None]
    for k in sequence:
        tiles = lax.all_gather(tiles, axes[k], axis=0, tiled=True)
    block = [lax.axis_size(axes[k]) for k in reversed(sequence)]
    tiles = tiles.reshape(*block, *x.shape)
    turned = sorted(range(len(sequence)), key=lambda place: sequence[len(sequence) - 1 - place])
    return tiles.transpose(*turned, *range(len(sequence), tiles.ndim)).reshape(-1, *x.shape)


def gather_axes(x, axes, sequence, dim):
    return in_order(gather_in_order(x, axes, sequence), dim)


def summed_rows(so_far, axes):
    for axis in axes:
        so_far = lax.psum_scatter(so_far, axis, scatter_dimension=0, tiled=True)
    return so_far


def dft_table(length):
    counter = jnp.arange(length, dtype=jnp.int32)
    product = counter[:, None] * counter[None, :] % length
    angle = product.astype(jnp.float32) * (-2.0 * jnp.pi / length)
    norm_scale = 1.0 / jnp.sqrt(jnp.float32(length))
    return (jnp.cos(angle) * norm_scale, jnp.sin(angle) * norm_scale)


def complex_mul(first_pair, second_pair):
    real_out = first_pair[0] * second_pair[0] - first_pair[1] * second_pair[1]
    imag_out = first_pair[0] * second_pair[1] + first_pair[1] * second_pair[0]
    return (real_out, imag_out)


def conjugate(grad_pair):
    return (grad_pair[0], -grad_pair[1])


def right_apply(field_pair, dft_pair):
    real_out = jnp.einsum(
        "pab,bc->pac", field_pair[0], dft_pair[0], precision=EXACT_MODE
    ) - jnp.einsum("pab,bc->pac", field_pair[1], dft_pair[1], precision=EXACT_MODE)
    imag_out = jnp.einsum(
        "pab,bc->pac", field_pair[0], dft_pair[1], precision=EXACT_MODE
    ) + jnp.einsum("pab,bc->pac", field_pair[1], dft_pair[0], precision=EXACT_MODE)
    return (real_out, imag_out)


def left_apply(dft_pair, field_pair):
    real_out = jnp.einsum(
        "ka,pac->pkc", dft_pair[0], field_pair[0], precision=EXACT_MODE
    ) - jnp.einsum("ka,pac->pkc", dft_pair[1], field_pair[1], precision=EXACT_MODE)
    imag_out = jnp.einsum(
        "ka,pac->pkc", dft_pair[1], field_pair[0], precision=EXACT_MODE
    ) + jnp.einsum("ka,pac->pkc", dft_pair[0], field_pair[1], precision=EXACT_MODE)
    return (real_out, imag_out)


def forward_dft(field_pair, dft_pair):
    rows_done = right_apply(field_pair, dft_pair)
    moved_pair = in_one_piece((rows_done[0], rows_done[1]), "col", 2, 1, 0)
    return left_apply(dft_pair, moved_pair)


def inverse_dft(field_pair, dft_conj):
    first_done = left_apply(dft_conj, field_pair)
    moved_pair = in_one_piece((first_done[0], first_done[1]), "col", 1, 2, 0)
    return right_apply(moved_pair, dft_conj)


def per_device(object_layers, probe_field, prop_phase, amplitude, offsets, counts):
    col_count = lax.axis_size("col")
    layer_count = object_layers.shape[0]
    tile_cols = object_layers.shape[3]
    full_cols = tile_cols * col_count
    slot_count = offsets.shape[0]
    patch_width = probe_field.shape[2]
    dft_pair = dft_table(patch_width)
    dft_conj = (dft_pair[0], -dft_pair[1])
    alive_mask = (jnp.arange(slot_count, dtype=jnp.int32) < counts[0]).astype(jnp.float32)
    row_at = offsets[:, 0]
    col_at = offsets[:, 1]
    strip_rows = gather_axes(object_layers, POS, (0, 1), 2)
    picked = jnp.stack([lax.dynamic_slice_in_dim(strip_rows, row_at[0], patch_width, 2)])
    part_rows = lax.all_to_all(picked, "col", split_axis=3, concat_axis=4, tiled=True)
    patches = jnp.stack([lax.dynamic_slice_in_dim(part_rows[0], col_at[0], patch_width, 3)])
    probe_pair = (probe_field[0][None], probe_field[1][None])
    kernel = (jnp.cos(prop_phase)[None], jnp.sin(prop_phase)[None])
    kernel_conj = (kernel[0], -kernel[1])
    layers_pair = [
        (patches[:, layer_idx, 0], patches[:, layer_idx, 1]) for layer_idx in range(layer_count)
    ]
    wave_now = complex_mul(probe_pair, layers_pair[0])
    layer_idx = 1
    spectrum = complex_mul(kernel, forward_dft(wave_now, dft_pair))
    propagated = inverse_dft(spectrum, dft_conj)
    wave_list = [propagated]
    wave_now = complex_mul(propagated, layers_pair[layer_idx])
    far_field = forward_dft(wave_now, dft_pair)
    modulus = jnp.maximum(
        jnp.sqrt(far_field[0] * far_field[0] + far_field[1] * far_field[1]), MOD_FLOOR
    )
    amp_ratio = amplitude / modulus
    residual = (far_field[0] - amp_ratio * far_field[0], far_field[1] - amp_ratio * far_field[1])
    backward = inverse_dft(residual, dft_conj)
    gradients = [None] * layer_count
    layer_idx = 1
    gradients[layer_idx] = complex_mul(conjugate(wave_list[layer_idx - 1]), backward)
    toward = complex_mul(conjugate(layers_pair[layer_idx]), backward)
    backward = inverse_dft(complex_mul(kernel_conj, forward_dft(toward, dft_pair)), dft_conj)
    gradients[0] = complex_mul(conjugate(probe_pair), backward)
    stacked = jnp.stack([jnp.stack(grad_pair, axis=1) for grad_pair in gradients], axis=1)
    stacked = stacked * alive_mask[:, None, None, None, None]
    wide_grad_shape = stacked.shape[1:4] + (full_cols,)
    tile_parts = jnp.stack(
        [
            lax.dynamic_update_slice_in_dim(
                jnp.zeros(wide_grad_shape, jnp.float32), stacked[0], col_at[0], 3
            )
        ]
    )
    arrived = lax.all_to_all(tile_parts, "col", split_axis=4, concat_axis=3, tiled=True)
    total_rows = strip_rows.shape[2]
    strip_term = jnp.zeros((total_rows, layer_count, 2, tile_cols), jnp.float32)
    moved_rows = jnp.transpose(arrived, (0, 3, 1, 2, 4))
    strip_term = lax.dynamic_update_slice_in_dim(strip_term, moved_rows[0], row_at[0], 0)
    summed = summed_rows(strip_term, POS)
    return jnp.transpose(summed, (1, 2, 0, 3))


def solution(mesh):
    finer = Mesh(mesh.devices.reshape(8, 12, mesh.shape["col"]), ("pos_0", "pos_1", "col"))
    return jax.shard_map(
        per_device,
        mesh=finer,
        in_specs=(
            P(None, None, POS, "col"),
            P(None, "col", None),
            P(None, "col"),
            P(POS, None, "col"),
            P(POS, None),
            P(POS),
        ),
        out_specs=P(None, None, POS, "col"),
        check_vma=False,
    )
```

profile of v0, /device:TPU:2, one launch (start us, length us, event | category | flops | bytes accessed | tf_op | source)
XLA Modules:
  0.0 372.7 jit_solution(16996795956070956509)
XLA Ops:
  6.5 28.4 %all-gather = f32[16,2,8,96]{3,2,1,0:T(8,128)} all-gather(f32[2,2,8,96]{3,2,1,0:T(8,128)} %param.6), channel_id=2, replica_groups=mesh['pos_0'=8,'pos_1'=12,'col'=8] {'pos_0'}, dimensions={0}, use_global_device_ids=true | all-gather | bytes 110592 | tf_op jit(solution)/shard_map/all_gather | solution.py:30
  35.0 1.3 fusion.330
  38.0 62.2 %all-gather.3.cloned.1.call-done = f32[96,2,2,8,96]{4,3,2,1,0:T(8,128)} async-done(((f32[8,2,2,8,96]{4,3,2,1,0:T(8,128)}), f32[96,2,2,8,96]{4,3,2,1,0:T(8,128)}) %all-gather.3.cloned.1.call-update) | async-done | bytes 1179664 | tf_op jit(solution)/shard_map/all_gather | solution.py:30
  100.3 1.6 copy.43
  103.2 4.8 %all-to-all-start = ((f32[1,2,2,256,96]{4,2,1,0,3:T(2,128)}), f32[1,2,2,256,96]{4,2,1,0,3:T(2,128)S(1)}, u32[]{:S(2)}, u32[]{:S(2)}) async-start(f32[1,2,2,256,96]{4,2,1,0,3:T(2,128)} %copy.46), calls=%async_computation | async-start | bytes 1048576 | tf_op jit(solution)/shard_map/all_to_all | solution.py:111
  110.0 6.9 %all-to-all-done = f32[1,2,2,256,96]{4,2,1,0,3:T(2,128)S(1)} async-done(((f32[1,2,2,256,96]{4,2,1,0,3:T(2,128)}), f32[1,2,2,256,96]{4,2,1,0,3:T(2,128)S(1)}, u32[]{:S(2)}, u32[]{:S(2)}) %all-to-all-start) | async-done | bytes 393248 | tf_op jit(solution)/shard_map/all_to_all | solution.py:111
  123.6 4.9 %all-to-all-start.1 = ((f32[8,1,2048]{2,1,0:T(1,128)}), f32[8,1,2048]{2,1,0:T(1,128)S(1)}, u32[]{:S(2)}, u32[]{:S(2)}) async-start(f32[8,1,2048]{2,1,0:T(1,128)} %reshape.319), calls=%async_computation.1 | async-start | bytes 131072 | tf_op jit(solution)/shard_map/all_to_all | solution.py:17
  128.7 4.0 %all-to-all-done.1 = f32[8,1,2048]{2,1,0:T(1,128)S(1)} async-done(((f32[8,1,2048]{2,1,0:T(1,128)}), f32[8,1,2048]{2,1,0:T(1,128)S(1)}, u32[]{:S(2)}, u32[]{:S(2)}) %all-to-all-start.1) | async-done | bytes 65568 | tf_op jit(solution)/shard_map/all_to_all | solution.py:17
  138.5 1.3 fusion.76
  145.5 8.2 %all_to_all.123 = f32[8,1,2048]{2,1,0:T(1,128)S(1)} all-to-all(f32[8,1,2048]{2,1,0:T(1,128)S(1)} %reshape.321), channel_id=1, replica_groups=mesh['pos_0'=8,'pos_1'=12,'col'=8] {'col'}, dimensions={0} | all-to-all | bytes 131072 | tf_op jit(solution)/shard_map/all_to_all | solution.py:17
  165.5 8.4 %all_to_all.124 = f32[8,1,2048]{2,1,0:T(1,128)S(1)} all-to-all(f32[8,1,2048]{2,1,0:T(1,128)S(1)} %reshape.323), channel_id=1, replica_groups=mesh['pos_0'=8,'pos_1'=12,'col'=8] {'col'}, dimensions={0} | all-to-all | bytes 131072 | tf_op jit(solution)/shard_map/all_to_all | solution.py:17
  186.3 8.2 %all_to_all.125 = f32[8,1,2048]{2,1,0:T(1,128)S(1)} all-to-all(f32[8,1,2048]{2,1,0:T(1,128)S(1)} %reshape.325), channel_id=1, replica_groups=mesh['pos_0'=8,'pos_1'=12,'col'=8] {'col'}, dimensions={0} | all-to-all | bytes 131072 | tf_op jit(solution)/shard_map/all_to_all | solution.py:17
  206.2 8.2 %all_to_all.126 = f32[8,1,2048]{2,1,0:T(1,128)S(1)} all-to-all(f32[8,1,2048]{2,1,0:T(1,128)S(1)} %reshape.327), channel_id=1, replica_groups=mesh['pos_0'=8,'pos_1'=12,'col'=8] {'col'}, dimensions={0} | all-to-all | bytes 131072 | tf_op jit(solution)/shard_map/all_to_all | solution.py:17
  219.8 1.3 fusion.70
  227.4 4.7 %all-to-all-start.6 = ((f32[8,1,2048]{2,1,0:T(1,128)}), f32[8,1,2048]{2,1,0:T(1,128)S(1)}, u32[]{:S(2)}, u32[]{:S(2)}) async-start(f32[8,1,2048]{2,1,0:T(1,128)} %reshape.329), calls=%async_computation.6 | async-start | bytes 131072 | tf_op jit(solution)/shard_map/all_to_all | solution.py:17
  233.0 3.3 all-to-all-done.6
  243.7 1.5 reshape.331
  245.2 11.3 %all_to_all.127 = f32[8,1,12288]{2,1,0:T(1,128)S(1)} all-to-all(f32[8,1,12288]{2,1,0:T(1,128)S(1)} %reshape.331), channel_id=1, replica_groups=mesh['pos_0'=8,'pos_1'=12,'col'=8] {'col'}, dimensions={0} | all-to-all | bytes 786432 | tf_op jit(solution)/shard_map/all_to_all | solution.py:148
  256.5 1.6 reduce.6
  258.1 1.3 reshape.332
  259.4 1.4 copy.67
  261.0 2.2 dynamic_update_slice.8
  264.5 41.8 %reduce-scatter.3.cloned.1.call-done = f32[96,2,2,96]{3,0,2,1:T(8,128)} async-done(((f32[768,2,2,96]{3,0,2,1:T(8,128)}), f32[96,2,2,96]{3,0,2,1:T(8,128)}) %reduce-scatter.3.cloned.1.call-update) | async-done | bytes 147472 | tf_op jit(solution)/shard_map/reduce_scatter | solution.py:43
  306.3 59.4 %reduce-scatter.5.cloned.1.call-done = f32[8,2,2,96]{3,0,2,1:T(8,128)} async-done(((f32[96,2,2,96]{3,0,2,1:T(8,128)}), f32[8,2,2,96]{3,0,2,1:T(8,128)}) %reduce-scatter.5.cloned.1.call-update) | async-done | bytes 12304 | tf_op jit(solution)/shard_map/reduce_scatter | solution.py:43
  (131 shorter events, 75.5 us)
Async XLA Ops:
  6.5 93.7 %all-gather.3.cloned.1.call-start = ((), (), s32[]{:S(2)}) async-start(), calls=%async_computation.10 | async-start | bytes 1703936 | tf_op jit(solution)/shard_map/all_gather | solution.py:30
  103.2 13.7 %all-to-all-start = ((f32[1,2,2,256,96]{4,2,1,0,3:T(2,128)}), f32[1,2,2,256,96]{4,2,1,0,3:T(2,128)S(1)}, u32[]{:S(2)}, u32[]{:S(2)}) async-start(f32[1,2,2,256,96]{4,2,1,0,3:T(2,128)} %copy.46), calls=%async_computation | async-start | bytes 1048576 | tf_op jit(solution)/shard_map/all_to_all | solution.py:111
  110.0 7.6 %copy-start.1 = (f32[2,32,256]{2,1,0:T(8,128)S(1)}, f32[2,32,256]{2,1,0:T(8,128)}, u32[]{:S(2)}) copy-start(f32[2,32,256]{2,1,0:T(8,128)} %param.7) | copy-start | bytes 196612
  120.1 8.5 %copy-start.2 = (f32[256,32]{0,1:T(8,128)S(1)}, f32[256,32]{0,1:T(8,128)}, u32[]{:S(2)}) copy-start(f32[256,32]{0,1:T(8,128)} %param.8) | copy-start | bytes 98308
  123.6 9.1 %all-to-all-start.1 = ((f32[8,1,2048]{2,1,0:T(1,128)}), f32[8,1,2048]{2,1,0:T(1,128)S(1)}, u32[]{:S(2)}, u32[]{:S(2)}) async-start(f32[8,1,2048]{2,1,0:T(1,128)} %reshape.319), calls=%async_computation.1 | async-start | bytes 131072 | tf_op jit(solution)/shard_map/all_to_all | solution.py:17
  176.5 4.0 %copy-start.3 = (f32[1,256,32]{1,2,0:T(8,128)S(1)}, f32[1,256,32]{1,2,0:T(8,128)}, u32[]{:S(2)}) copy-start(f32[1,256,32]{1,2,0:T(8,128)} %param.9) | copy-start | bytes 98308
  227.4 8.9 %all-to-all-start.6 = ((f32[8,1,2048]{2,1,0:T(1,128)}), f32[8,1,2048]{2,1,0:T(1,128)S(1)}, u32[]{:S(2)}, u32[]{:S(2)}) async-start(f32[8,1,2048]{2,1,0:T(1,128)} %reshape.329), calls=%async_computation.6 | async-start | bytes 131072 | tf_op jit(solution)/shard_map/all_to_all | solution.py:17
  232.1 74.2 %reduce-scatter.3.cloned.1.call-start = ((), (), s32[]{:S(2)}) async-start(), calls=%async_computation.11 | async-start | bytes 1769472 | tf_op jit(solution)/shard_map/reduce_scatter | solution.py:43
  263.3 1.1 copy-start
  264.4 101.3 %reduce-scatter.5.cloned.1.call-start = ((), (), s32[]{:S(2)}) async-start(), calls=%async_computation.12 | async-start | bytes 212992 | tf_op jit(solution)/shard_map/reduce_scatter | solution.py:43
Sparse Core Ops, SparseCore 0:
  35.1 65.1 all-gather.2
  264.5 41.7 reduce-scatter.2
  309.4 56.2 reduce-scatter.4
where the time goes:
time: 379 us; the launch traced here: 373 us
  waiting for transfers between devices  178 us (47%)
  blocking collectives  72.7 us (19%)
  matrix products  60.7 us (16%)
  local copies, waits for them, and re-layouts  21.7 us (6%)
  between operations  18.8 us (5%)
  starting transfers between devices  14.7 us (4%)
  other arithmetic  6.46 us (2%)
    reduce_scatter x2, waiting for transfers between devices, summed_rows(): so_far = lax.psum_scatter(so_far, axis, scatter_dimension=0, tiled=True)  101 us
    all_gather x1, waiting for transfers between devices, gather_in_order(): tiles = lax.all_gather(tiles, axes[k], axis=0, tiled=True)  62.2 us
    all_to_all x4, blocking collectives, in_one_piece(): lax.all_to_all(both, axis, split_axis=split_dim, concat_axis=concat_dim,...  33 us
    all_gather x1, blocking collectives, gather_in_order(): tiles = lax.all_gather(tiles, axes[k], axis=0, tiled=True)  28.4 us
    all_to_all x1, blocking collectives, per_device(): lax.all_to_all(tile_parts, 'col', split_axis=4, concat_axis=3, tiled=True)  11.3 us
    all_to_all x2, starting transfers between devices, in_one_piece(): lax.all_to_all(both, axis, split_axis=split_dim, concat_axis=concat_dim,...  9.64 us
    unnamed x22, local copies, waits for them, and re-layouts  8.32 us
    dot_general x6, matrix products, left_apply(): jnp.einsum('ka,pac->pkc', dft_pair[1], field_pair[1], precision=EXACT_MODE)  7.81 us
  transfers between devices with their start and end apart: 6, of which 6 were waited for; matrix products, arithmetic and copies ran while one was open for 0% of the time, Pallas kernels for 0%

commit v1 on v0

v1 whole, which is shorter than its diff:
```python
import functools

import jax
import jax.numpy as jnp
import numpy as np
from jax import lax
from jax.experimental import pallas as pl
from jax.experimental.pallas import tpu as pltpu
from jax.sharding import Mesh
from jax.sharding import PartitionSpec as P

POS = ("pos_0", "pos_1")
MOD_FLOOR = 0.1

Y, Z, C = 8, 12, 8
N = 256
PLANES = 4
TILE = 8
CLASS_IN_STRIP = 12
CLASS_IN_PATCH = 32
TILES_PER_Z = 3
LANES = 128
VMEM_LIMIT = 60 * 1024 * 1024
F32 = jnp.float32
BF16 = jnp.bfloat16


def exchange(x, axes):
    return lax.all_to_all(x, axes, 0, 0, tiled=True)


def class_order():
    table = np.zeros((C * CLASS_IN_STRIP, LANES), np.float32)
    for j in range(C):
        for u in range(CLASS_IN_STRIP):
            table[C * u + j, 16 * j + u] = 1.0
    return table


def dft_tables():
    counter = np.arange(N)
    angle = (counter[:, None] * counter[None, :] % N) * (2.0 * np.pi / N)
    cosine, sine = np.cos(angle) / 16.0, np.sin(angle) / 16.0
    parts = []
    for table in (cosine, cosine + sine, cosine - sine):
        table = table.astype(np.float32)
        high = table.astype(jnp.bfloat16)
        low = (table - high.astype(np.float32)).astype(jnp.bfloat16)
        parts += [high, low]
    return np.stack(parts)


def lanes():
    return lax.broadcasted_iota(jnp.int32, (TILE, LANES), 1)


def between(lane, low, width):
    return (lane >= low) & (lane < low + width)


def rolled(x, shift):
    if isinstance(shift, int):
        shift = shift % LANES
        return pltpu.roll(x, shift, 1) if shift else x
    return pltpu.roll(x, lax.rem(shift + LANES, LANES), 1)


def split_kernel(x_ref, order_ref, o_ref):
    tile = x_ref[...].reshape(PLANES * TILE, C * CLASS_IN_STRIP)
    ordered = jnp.dot(
        tile, order_ref[...], precision=lax.Precision.HIGHEST, preferred_element_type=F32
    )
    lane = lanes()
    for j in range(C):
        piece = jnp.zeros((TILE, LANES), F32)
        for p in range(PLANES):
            moved = rolled(ordered[p * TILE : (p + 1) * TILE], 32 * p - 16 * j)
            piece = jnp.where(between(lane, 32 * p, CLASS_IN_STRIP), moved, piece)
        for y in range(Y):
            o_ref[y * C + j] = piece


def window(off_ref, me_ref, z):
    row, col = off_ref[z, 0], off_ref[z, 1]
    z_me, c_me = me_ref[0], me_ref[1]
    first = lax.shift_right_logical(row, 3)
    ahead = lax.rem(z_me - first + 6 * Z, Z)
    y_first = lax.div(first + ahead - z_me, Z)
    u_first = lax.shift_right_logical(col - c_me + 7, 3)
    return y_first, u_first


def select_kernel(off_ref, me_ref, x_ref, o_ref, strip_ref):
    lane = lanes()
    for y in range(Y):
        for p in range(PLANES):
            line = jnp.zeros((TILE, LANES), F32)
            for j in range(C):
                moved = rolled(x_ref[y * C + j], CLASS_IN_STRIP * j - 32 * p)
                line = jnp.where(between(lane, CLASS_IN_STRIP * j, CLASS_IN_STRIP), moved, line)
            strip_ref[p, y] = line
    for p in range(PLANES):
        strip_ref[p, Y] = jnp.zeros((TILE, LANES), F32)
    for z in range(Z):
        y_first, u_first = window(off_ref, me_ref, z)
        for k in range(TILES_PER_Z):
            piece = jnp.zeros((TILE, LANES), F32)
            for p in range(PLANES):
                moved = rolled(strip_ref[p, y_first + k], 32 * p - u_first)
                piece = jnp.where(between(lane, 32 * p, CLASS_IN_PATCH), moved, piece)
            o_ref[z, k * TILE : (k + 1) * TILE] = piece


def pack_kernel(own_ref, x_ref, phase_ref, amp_ref, probe_ref, o_ref, rows_ref):
    row = own_ref[0]
    first = lax.shift_right_logical(row, 3)
    for m in range(Z * TILES_PER_Z):
        k = m // Z
        rows_ref[m * TILE : (m + 1) * TILE] = x_ref[
            lax.rem(first + m, Z), k * TILE : (k + 1) * TILE
        ]
    patch = rows_ref[pl.ds(row & 7, N), :].T
    for copy in range(C):
        o_ref[copy, 0:128] = patch
        o_ref[copy, 128:160] = phase_ref[...]
        o_ref[copy, 160:192] = amp_ref[...]
        o_ref[copy, 192:224] = probe_ref[0]
        o_ref[copy, 224:256] = probe_ref[1]


def two_terms(x):
    high = x.astype(BF16)
    return high, (x - high.astype(F32)).astype(BF16)


def product(first, second):
    def dot(a, b):
        return jnp.dot(a, b, preferred_element_type=F32)

    return dot(first[0], second[0]) + (dot(first[0], second[1]) + dot(first[1], second[0]))


def store(ref, at, value):
    ref[at, 0] = value[:, :LANES]
    ref[at, 1] = value[:, LANES:]


def load(ref, at, rows=slice(None)):
    return jnp.concatenate([ref[at, 0, rows, :], ref[at, 1, rows, :]], axis=1)


def main_kernel(
    own_ref, me_ref, g_ref, tab_ref, o_ref, patch_ref, h_ref, amp_ref, probe_ref, wave_ref, x_ref, rows_ref
):
    row, col, count = own_ref[0], own_ref[1], own_ref[2]
    for s in range(C):
        source = lax.rem(col + s, C)
        for p in range(PLANES):
            for half in range(2):
                patch_ref[p, half, pl.ds(s, CLASS_IN_PATCH, stride=C), :] = g_ref[
                    source, p * 32 : (p + 1) * 32, half * LANES : (half + 1) * LANES
                ]
    phase = g_ref[:, 128:160, :].reshape(N, N)
    store(h_ref, 0, jnp.cos(phase))
    store(h_ref, 1, jnp.sin(phase))
    amp_ref[...] = g_ref[:, 160:192, :].reshape(N, N)
    store(probe_ref, 0, g_ref[:, 192:224, :].reshape(N, N).T)
    store(probe_ref, 1, g_ref[:, 224:256, :].reshape(N, N).T)

    def table(k):
        return tab_ref[2 * k], tab_ref[2 * k + 1]

    def held(ref, at=0, rows=slice(None)):
        return load(ref, at, rows), load(ref, at + 1, rows)

    def keep(ref, pair):
        store(ref, 0, pair[0])
        store(ref, 1, pair[1])

    def transform(pair, inverse):
        real_table, imag_table = (1, 2) if inverse else (2, 1)
        for left in (False, True):
            real, imag = pair
            both = two_terms(real + imag)
            real, imag = two_terms(real), two_terms(imag)

            def times(data, k):
                return product(table(k), data) if left else product(data, table(k))

            common = times(both, 0)
            keep(x_ref, (common - times(imag, real_table), common - times(real, imag_table)))
            pair = held(x_ref)
        return pair

    def times(a, b):
        return a[0] * b[0] - a[1] * b[1], a[0] * b[1] + a[1] * b[0]

    def conj_times(a, b):
        return a[0] * b[0] + a[1] * b[1], a[0] * b[1] - a[1] * b[0]

    spectrum = transform(times(held(probe_ref), held(patch_ref)), False)
    wave = transform(times(held(h_ref), spectrum), True)
    keep(wave_ref, wave)
    far = transform(times(held(wave_ref), held(patch_ref, 2)), False)
    modulus = jnp.maximum(jnp.sqrt(far[0] * far[0] + far[1] * far[1]), MOD_FLOOR)
    ratio = amp_ref[...] / modulus
    back = transform((far[0] - ratio * far[0], far[1] - ratio * far[1]), True)
    keep(wave_ref, conj_times(held(wave_ref), back))
    toward = transform(conj_times(held(patch_ref, 2), back), False)
    transform(conj_times(held(h_ref), toward), True)

    mine = pl.ds(lax.rem(me_ref[1] - col + 1024, C), CLASS_IN_PATCH, stride=C)
    first_grad = conj_times(held(probe_ref, 0, mine), held(x_ref, 0, mine))
    second_grad = held(wave_ref, 0, mine)
    alive = (count > 0).astype(F32)
    grads = jnp.concatenate([*first_grad, *second_grad], axis=0) * alive
    rows_ref[...] = jnp.zeros_like(rows_ref)
    rows_ref[pl.ds(row & 7, N), :] = grads.T
    first = lax.shift_right_logical(row, 3)
    for m in range(Z * TILES_PER_Z):
        k = m // Z
        o_ref[lax.rem(first + m, Z), k * TILE : (k + 1) * TILE] = rows_ref[
            m * TILE : (m + 1) * TILE
        ]


def gather_kernel(off_ref, me_ref, x_ref, o_ref, sum_ref):
    lane = lanes()
    sum_ref[...] = jnp.zeros_like(sum_ref)
    for z in range(Z):
        y_first, u_first = window(off_ref, me_ref, z)
        inside = between(lane, u_first, CLASS_IN_PATCH)
        for k in range(TILES_PER_Z):
            piece = x_ref[z, k * TILE : (k + 1) * TILE]
            for p in range(PLANES):
                moved = jnp.where(inside, rolled(piece, u_first - 32 * p), 0.0)
                sum_ref[p, y_first + k] += moved
    for y in range(Y):
        for j in range(C):
            piece = jnp.zeros((TILE, LANES), F32)
            for p in range(PLANES):
                moved = rolled(sum_ref[p, y], 32 * p - CLASS_IN_STRIP * j)
                piece = jnp.where(between(lane, 32 * p, CLASS_IN_STRIP), moved, piece)
            o_ref[y * C + j] = piece


def merge_kernel(x_ref, order_ref, o_ref):
    lane = lanes()
    sums = []
    for j in range(C):
        total = x_ref[j]
        for y in range(1, Y):
            total = total + x_ref[y * C + j]
        sums.append(total)
    planes = []
    for p in range(PLANES):
        line = jnp.zeros((TILE, LANES), F32)
        for j in range(C):
            line = jnp.where(
                between(lane, 16 * j, CLASS_IN_STRIP), rolled(sums[j], 16 * j - 32 * p), line
            )
        planes.append(line)
    ordered = jnp.concatenate(planes, axis=0)
    tile = jnp.dot(
        ordered, order_ref[...], precision=lax.Precision.HIGHEST, preferred_element_type=F32
    )
    o_ref[...] = tile.reshape(2, 2, TILE, C * CLASS_IN_STRIP)


IN_VMEM = pl.BlockSpec(memory_space=pltpu.VMEM)
IN_SMEM = pl.BlockSpec(memory_space=pltpu.SMEM)


def call(kernel, out_shape, scalars, arrays, scratch=()):
    return pl.pallas_call(
        kernel,
        out_shape=jax.ShapeDtypeStruct(out_shape, F32),
        in_specs=[IN_SMEM] * len(scalars) + [IN_VMEM] * len(arrays),
        out_specs=IN_VMEM,
        scratch_shapes=[pltpu.VMEM(shape, F32) for shape in scratch],
        compiler_params=pltpu.CompilerParams(vmem_limit_bytes=VMEM_LIMIT),
    )(*scalars, *arrays)


def per_device(object_layers, probe_field, prop_phase, amplitude, offsets, counts):
    order = class_order()
    me = jnp.stack([lax.axis_index("pos_1"), lax.axis_index("col")]).astype(jnp.int32)
    own = jnp.concatenate([offsets[0], counts])
    line_offsets = exchange(jnp.broadcast_to(offsets[None], (Z, 1, 2)), "pos_1").reshape(Z, 2)
    split = call(split_kernel, (Y * C, TILE, LANES), (), (object_layers, jnp.asarray(order)))
    columns = exchange(split, ("pos_0", "col"))
    strip_shape = (PLANES, Y + 1, TILE, LANES)
    piece_shape = (Z, TILES_PER_Z * TILE, LANES)
    halves = (2, N, LANES)
    rows_shape = (Z * TILES_PER_Z * TILE + TILE, LANES)
    chosen = call(select_kernel, piece_shape, (line_offsets, me), (columns,), (strip_shape,))
    rows = exchange(chosen, "pos_1")
    packed = call(
        pack_kernel,
        (C, N, N),
        (own,),
        (rows, prop_phase.T, amplitude[0].T, probe_field),
        (rows_shape,),
    )
    gathered = exchange(packed, "col")
    grads = call(
        main_kernel,
        piece_shape,
        (own, me),
        (gathered, jnp.asarray(dft_tables())),
        ((4, *halves), (2, *halves), (N, N), (2, *halves), (2, *halves), (2, *halves), rows_shape),
    )
    returned = exchange(grads, "pos_1")
    summed = call(gather_kernel, (Y * C, TILE, LANES), (line_offsets, me), (returned,), (strip_shape,))
    tiles = exchange(summed, ("pos_0", "col"))
    return call(merge_kernel, (2, 2, TILE, C * CLASS_IN_STRIP), (), (tiles, jnp.asarray(order.T)))


def solution(mesh):
    finer = Mesh(mesh.devices.reshape(Y, Z, C), ("pos_0", "pos_1", "col"))
    return jax.shard_map(
        per_device,
        mesh=finer,
        in_specs=(
            P(None, None, POS, "col"),
            P(None, "col", None),
            P(None, "col"),
            P(POS, None, "col"),
            P(POS, None),
            P(POS),
        ),
        out_specs=P(None, None, POS, "col"),
        check_vma=False,
    )
```

time: 379 us -> 156 us (0.41)
  the two profiles are of different devices: /device:TPU:2 before, /device:TPU:1 now
where the time goes in v1:
time: 156 us; the launch traced here: 155 us
  blocking collectives  68.5 us (44%)
  starting transfers between devices  31.4 us (20%)
  waiting for transfers between devices  28.6 us (18%)
  Pallas kernels  20.5 us (13%)
  local copies, waits for them, and re-layouts  3.38 us (2%)
  other arithmetic  1.87 us (1%)
    all_to_all x3, blocking collectives, exchange(): return lax.all_to_all(x, axes, 0, 0, tiled=True)  68.5 us
    all_to_all x3, starting transfers between devices, exchange(): return lax.all_to_all(x, axes, 0, 0, tiled=True)  31.4 us
    all_to_all x3, waiting for transfers between devices, exchange(): return lax.all_to_all(x, axes, 0, 0, tiled=True)  28.6 us
    pallas_call x6, Pallas kernels, call(): pl.pallas_call(kernel, out_shape=jax.ShapeDtypeStruct(out_shape, F32), in...  20.5 us
  transfers between devices with their start and end apart: 3, of which 3 were waited for; matrix products, arithmetic and copies ran while one was open for 2% of the time, Pallas kernels for 1%

profile of v1, /device:TPU:1, one launch (start us, length us, event | category | flops | bytes accessed | tf_op | source)
XLA Modules:
  0.0 155.0 jit_solution(2792371571005980753)
XLA Ops:
  0.0 1.3 broadcast_in_dim.9
  1.3 15.7 %all-to-all-start = ((s32[12,1,2]{2,1,0:T(1,128)}), s32[12,1,2]{2,1,0:T(1,128)S(1)}, u32[]{:S(2)}, u32[]{:S(2)}) async-start(s32[12,1,2]{2,1,0:T(1,128)} %broadcast_in_dim.9), calls=%async_computation | async-start | bytes 12288 | tf_op jit(solution)/shard_map/all_to_all | solution.py:29
  17.0 1.8 %shard_map.91 = f32[64,8,128]{2,1,0:T(8,128)} custom-call(f32[2,2,8,96]{3,2,1,0:T(8,128)} %x_ref.1, f32[96,128]{1,0:T(8,128)} %constant.14.clone.order_ref), custom_call_target="tpu_custom_call" | custom-call | tf_op jit(solution)/shard_map/pallas_call | solution.py:275
  18.7 7.1 %all-to-all-done = s32[12,1,2]{2,1,0:T(1,128)S(1)} async-done(((s32[12,1,2]{2,1,0:T(1,128)}), s32[12,1,2]{2,1,0:T(1,128)S(1)}, u32[]{:S(2)}, u32[]{:S(2)}) %all-to-all-start) | async-done | bytes 128 | tf_op jit(solution)/shard_map/all_to_all | solution.py:29
  25.8 12.2 %all-to-all-start.1 = ((f32[64,8,128]{2,1,0:T(8,128)}), f32[64,8,128]{2,1,0:T(8,128)S(1)}, u32[]{:S(2)}, u32[]{:S(2)}) async-start(f32[64,8,128]{2,1,0:T(8,128)} %shard_map.91), calls=%async_computation.1 | async-start | bytes 524288 | tf_op jit(solution)/shard_map/all_to_all | solution.py:29
  38.1 0.6 pad_add_fusion.me_ref
  38.7 0.1 copy.12
  38.8 0.7 copy.14.off_ref
  39.5 11.7 %all-to-all-done.1.x_ref = f32[64,8,128]{2,1,0:T(8,128)S(1)} async-done(((f32[64,8,128]{2,1,0:T(8,128)}), f32[64,8,128]{2,1,0:T(8,128)S(1)}, u32[]{:S(2)}, u32[]{:S(2)}) %all-to-all-start.1) | async-done | bytes 262176 | tf_op jit(solution)/shard_map/all_to_all | solution.py:29
  51.1 0.0 copy-start
  51.1 0.7 copy-done
  51.8 2.2 %shard_map.92 = f32[12,24,128]{2,1,0:T(8,128)} custom-call(s32[12,2]{1,0:T(8,128)} %copy.14.off_ref, s32[2]{0:T(128)} %pad_add_fusion.me_ref, f32[64,8,128]{2,1,0:T(8,128)} %copy-done), custom_call_target="tpu_custom_call" | custom-call | tf_op jit(solution)/shard_map/pallas_call | solution.py:275
  54.0 3.5 %all-to-all-start.2 = ((f32[12,24,128]{2,1,0:T(8,128)}), f32[12,24,128]{2,1,0:T(8,128)S(1)}, u32[]{:S(2)}, u32[]{:S(2)}) async-start(f32[12,24,128]{2,1,0:T(8,128)} %shard_map.92), calls=%async_computation.2 | async-start | bytes 294912 | tf_op jit(solution)/shard_map/all_to_all | solution.py:29
  58.2 1.3 pad_add_fusion.1.own_ref
  59.4 9.9 %all-to-all-done.2.x_ref = f32[12,24,128]{2,1,0:T(8,128)S(1)} async-done(((f32[12,24,128]{2,1,0:T(8,128)}), f32[12,24,128]{2,1,0:T(8,128)S(1)}, u32[]{:S(2)}, u32[]{:S(2)}) %all-to-all-start.2) | async-done | bytes 147488 | tf_op jit(solution)/shard_map/all_to_all | solution.py:29
  69.3 0.0 copy-start.1
  69.3 0.7 copy-done.1
  70.0 2.5 %shard_map.93 = f32[8,256,256]{2,1,0:T(8,128)} custom-call(s32[3]{0:T(128)} %pad_add_fusion.1.own_ref, f32[12,24,128]{2,1,0:T(8,128)} %copy-done.1, f32[32,256]{1,0:T(8,128)} %bitcast.8, f32[32,256]{1,0:T(8,128)} %bitcast.9, f32[2,32,256]{2,1,0:T(8,128)} %probe_ref.1), custom_call_target="tpu_custom_call" | custom-call | tf_op jit(solution)/shard_map/pallas_call | solution.py:275
  72.4 33.0 %all_to_all.30.g_ref = f32[8,256,256]{2,1,0:T(8,128)} all-to-all(f32[8,256,256]{2,1,0:T(8,128)} %shard_map.93), channel_id=1, replica_groups=mesh['pos_0'=8,'pos_1'=12,'col'=8] {'col'}, dimensions={0} | all-to-all | bytes 4194304 | tf_op jit(solution)/shard_map/all_to_all | solution.py:29
  105.4 10.1 %shard_map.94 = f32[12,24,128]{2,1,0:T(8,128)} custom-call(s32[3]{0:T(128)} %pad_add_fusion.1.own_ref, s32[2]{0:T(128)} %pad_add_fusion.me_ref, f32[8,256,256]{2,1,0:T(8,128)} %all_to_all.30.g_ref, bf16[6,256,256]{2,1,0:T(8,128)(2,1)} %constant.15.clone.tab_ref), custom_call_target="tpu_custom_call" | custom-call | tf_op jit(solution)/shard_map/pallas_call | solution.py:275
  115.5 14.9 %all_to_all.31.x_ref = f32[12,24,128]{2,1,0:T(8,128)} all-to-all(f32[12,24,128]{2,1,0:T(8,128)} %shard_map.94), channel_id=1, replica_groups=mesh['pos_0'=8,'pos_1'=12,'col'=8] {'pos_1'}, dimensions={0} | all-to-all | bytes 294912 | tf_op jit(solution)/shard_map/all_to_all | solution.py:29
  130.4 2.2 %shard_map.95 = f32[64,8,128]{2,1,0:T(8,128)} custom-call(s32[12,2]{1,0:T(8,128)} %copy.14.off_ref, s32[2]{0:T(128)} %pad_add_fusion.me_ref, f32[12,24,128]{2,1,0:T(8,128)} %all_to_all.31.x_ref), custom_call_target="tpu_custom_call" | custom-call | tf_op jit(solution)/shard_map/pallas_call | solution.py:275
  132.6 20.6 %all_to_all.32.x_ref = f32[64,8,128]{2,1,0:T(8,128)} all-to-all(f32[64,8,128]{2,1,0:T(8,128)} %shard_map.95), channel_id=1, replica_groups=mesh['pos_0'=8,'pos_1'=12,'col'=8] {'pos_0','col'}, dimensions={0} | all-to-all | bytes 524288 | tf_op jit(solution)/shard_map/all_to_all | solution.py:29
  153.2 1.8 %shard_map.96 = f32[2,2,8,96]{3,2,1,0:T(8,128)} custom-call(f32[64,8,128]{2,1,0:T(8,128)} %all_to_all.32.x_ref, f32[128,96]{1,0:T(8,128)} %constant.16.clone.order_ref), custom_call_target="tpu_custom_call" | custom-call | tf_op jit(solution)/shard_map/pallas_call | solution.py:275
Async XLA Ops:
  1.3 24.6 %all-to-all-start = ((s32[12,1,2]{2,1,0:T(1,128)}), s32[12,1,2]{2,1,0:T(1,128)S(1)}, u32[]{:S(2)}, u32[]{:S(2)}) async-start(s32[12,1,2]{2,1,0:T(1,128)} %broadcast_in_dim.9), calls=%async_computation | async-start | bytes 12288 | tf_op jit(solution)/shard_map/all_to_all | solution.py:29
  25.8 25.3 %all-to-all-start.1 = ((f32[64,8,128]{2,1,0:T(8,128)}), f32[64,8,128]{2,1,0:T(8,128)S(1)}, u32[]{:S(2)}, u32[]{:S(2)}) async-start(f32[64,8,128]{2,1,0:T(8,128)} %shard_map.91), calls=%async_computation.1 | async-start | bytes 524288 | tf_op jit(solution)/shard_map/all_to_all | solution.py:29
  51.1 0.7 copy-start
  54.0 15.3 %all-to-all-start.2 = ((f32[12,24,128]{2,1,0:T(8,128)}), f32[12,24,128]{2,1,0:T(8,128)S(1)}, u32[]{:S(2)}, u32[]{:S(2)}) async-start(f32[12,24,128]{2,1,0:T(8,128)} %shard_map.92), calls=%async_computation.2 | async-start | bytes 294912 | tf_op jit(solution)/shard_map/all_to_all | solution.py:29
  69.3 0.7 copy-start.1

commit v2 on v1

v2 whole, which is shorter than its diff:
```python
import jax
import jax.numpy as jnp
import numpy as np
from jax import lax
from jax.experimental import pallas as pl
from jax.experimental.pallas import tpu as pltpu
from jax.sharding import Mesh
from jax.sharding import PartitionSpec as P

POS = ("pos_0", "pos_1")
MOD_FLOOR = 0.1

Y, Z, C = 8, 12, 8
CHIPS, CORES = 4, 2
N = 256
PLANES = 4
TILE = 8
CLASS_IN_STRIP = 12
CLASS_IN_PATCH = 32
TILES_PER_Z = 3
LANES = 128
F32 = jnp.float32
BF16 = jnp.bfloat16


def exchange(x, axes):
    return lax.all_to_all(x, axes, 0, 0, tiled=True)


def class_order():
    table = np.zeros((C * CLASS_IN_STRIP, LANES), np.float32)
    for j in range(C):
        for u in range(CLASS_IN_STRIP):
            table[C * u + j, 16 * j + u] = 1.0
    return table


def dft_tables():
    counter = np.arange(N)
    angle = (counter[:, None] * counter[None, :] % N) * (2.0 * np.pi / N)
    cosine, sine = np.cos(angle) / 16.0, np.sin(angle) / 16.0
    parts = []
    for table in (cosine, cosine + sine, cosine - sine):
        table = table.astype(np.float32)
        high = table.astype(jnp.bfloat16)
        low = (table - high.astype(np.float32)).astype(jnp.bfloat16)
        parts += [high, low]
    return np.stack(parts)


def lanes():
    return lax.broadcasted_iota(jnp.int32, (TILE, LANES), 1)


def between(lane, low, width):
    return (lane >= low) & (lane < low + width)


def rolled(x, shift):
    if isinstance(shift, int):
        shift = shift % LANES
        return pltpu.roll(x, shift, 1) if shift else x
    return pltpu.roll(x, (shift + 2 * LANES) & (LANES - 1), 1)


def spread_masks(shift):
    lane = lanes()
    row = lax.broadcasted_iota(jnp.int32, (TILE, LANES), 0)
    base = lane - jnp.where(row < 4, 0, 16) - shift + 4 * LANES
    return [((base - 32 * p) & (LANES - 1)) < CLASS_IN_STRIP for p in range(PLANES)]


def upper_half():
    return lax.broadcasted_iota(jnp.int32, (TILE, LANES), 0) < 4


def folded(piece):
    return (piece + pltpu.roll(piece, 4, 0))[:4]


def unfolded(piece):
    return jnp.concatenate([piece, piece], axis=0)


def two_shifts(x, shift, low):
    return jnp.where(low, rolled(x, shift), rolled(x, shift + 16))


def split_kernel(me_ref, x_ref, order_ref, o_ref):
    shift = CLASS_IN_STRIP * me_ref[1]
    tile = x_ref[...].reshape(PLANES * TILE, C * CLASS_IN_STRIP)
    ordered = jnp.dot(
        tile, order_ref[...], precision=lax.Precision.HIGHEST, preferred_element_type=F32
    )
    masks, low = spread_masks(shift), upper_half()
    for j in range(C):
        piece = jnp.zeros((TILE, LANES), F32)
        for p in range(PLANES):
            moved = two_shifts(ordered[p * TILE : (p + 1) * TILE], shift + 32 * p - 16 * j, low)
            piece = jnp.where(masks[p], moved, piece)
        piece = folded(piece)
        for y in range(Y):
            o_ref[y * C + j] = piece


def window(off_ref, me_ref, z):
    row, col = off_ref[z, 0, 0], off_ref[z, 0, 1]
    z_me, c_me = me_ref[0], me_ref[1]
    first = lax.shift_right_logical(row, 3)
    ahead = lax.rem(z_me - first + 6 * Z, Z)
    y_first = lax.div(first + ahead - z_me, Z)
    u_first = lax.shift_right_logical(col - c_me + 7, 3)
    return y_first, u_first


def select_kernel(off_ref, me_ref, x_ref, o_ref, strip_ref):
    lane, low = lanes(), upper_half()
    masks = [spread_masks(CLASS_IN_STRIP * j) for j in range(C)]
    for y in range(Y):
        pieces = [unfolded(x_ref[y * C + j]) for j in range(C)]
        for p in range(PLANES):
            line = pieces[0]
            for j in range(1, C):
                line = jnp.where(masks[j][p], pieces[j], line)
            strip_ref[p, y] = jnp.where(low, rolled(line, -32 * p), rolled(line, -32 * p - 16))
    for p in range(PLANES):
        strip_ref[p, Y] = jnp.zeros((TILE, LANES), F32)
    for z in range(Z):
        y_first, u_first = window(off_ref, me_ref, z)
        for k in range(TILES_PER_Z):
            piece = rolled(strip_ref[0, y_first + k], LANES - u_first)
            for p in range(1, PLANES):
                moved = rolled(strip_ref[p, y_first + k], 32 * p - u_first)
                piece = jnp.where(lane >= 32 * p, moved, piece)
            o_ref[z, k * TILE : (k + 1) * TILE] = piece


def pack_kernel(own_ref, x_ref, phase_ref, amp_ref, probe_ref, o_ref, rows_ref):
    row = own_ref[0, 0]
    first = lax.shift_right_logical(row, 3)
    for m in range(Z * TILES_PER_Z):
        k = m // Z
        rows_ref[m * TILE : (m + 1) * TILE] = x_ref[
            lax.rem(first + m, Z), k * TILE : (k + 1) * TILE
        ]
    patch = rows_ref[pl.ds(row & 7, N), :].T
    for copy in range(CHIPS):
        o_ref[copy, 0:128] = patch
        o_ref[copy, 128:160] = phase_ref[...]
        o_ref[copy, 160:192] = amp_ref[...]
        o_ref[copy, 192:224] = probe_ref[0]
        o_ref[copy, 224:256] = probe_ref[1]


def two_terms(x):
    high = x.astype(BF16)
    return high, (x - high.astype(F32)).astype(BF16)


def product(first, second):
    return jnp.dot(
        jnp.concatenate([first[0], first[0], first[1]], axis=1),
        jnp.concatenate([second[0], second[1], second[0]], axis=0),
        preferred_element_type=F32,
    )


def store(ref, at, value):
    ref[at, 0] = value[:, :LANES]
    ref[at, 1] = value[:, LANES:]


def load(ref, at, rows=slice(None)):
    return jnp.concatenate([ref[at, 0, rows, :], ref[at, 1, rows, :]], axis=1)


def main_kernel(
    own_ref, count_ref, me_ref, g_ref, other_ref, tab_ref, o_ref,
    patch_ref, h_ref, amp_ref, raw_ref, probe_ref, wave_ref, x_ref, rows_ref,
):
    row, col = own_ref[0, 0], own_ref[0, 1]
    core = me_ref[1] & 1
    for source_ref, core_of in ((g_ref, core), (other_ref, 1 - core)):
        for chip in range(CHIPS):
            j = CORES * chip + core_of
            s = (j - col + 1024) & (C - 1)
            mine = pl.ds(pl.multiple_of(32 * j, 32), 32)
            phase = source_ref[chip, 128:160, :]
            cosine, sine = jnp.cos(phase), jnp.sin(phase)
            amp_ref[mine, :] = source_ref[chip, 160:192, :]
            raw_ref[0, mine, :] = source_ref[chip, 192:224, :]
            raw_ref[1, mine, :] = source_ref[chip, 224:256, :]
            for half in range(2):
                part = slice(half * LANES, (half + 1) * LANES)
                h_ref[0, half, mine, :] = cosine[:, part]
                h_ref[1, half, mine, :] = sine[:, part]
                for p in range(PLANES):
                    patch_ref[p, half, pl.ds(s, CLASS_IN_PATCH, stride=C), :] = source_ref[
                        chip, p * 32 : (p + 1) * 32, part
                    ]
    store(probe_ref, 0, raw_ref[0].T)
    store(probe_ref, 1, raw_ref[1].T)

    def table(k):
        return tab_ref[2 * k], tab_ref[2 * k + 1]

    def held(ref, at=0, rows=slice(None)):
        return load(ref, at, rows), load(ref, at + 1, rows)

    def keep(ref, pair):
        store(ref, 0, pair[0])
        store(ref, 1, pair[1])

    def stage(pair, inverse, left):
        real_table, imag_table = (1, 2) if inverse else (2, 1)
        real, imag = pair
        both = two_terms(real + imag)
        real, imag = two_terms(real), two_terms(imag)

        def times(data, k):
            return product(table(k), data) if left else product(data, table(k))

        common = times(both, 0)
        return common - times(imag, real_table), common - times(real, imag_table)

    def transform(pair, inverse):
        keep(x_ref, stage(pair, inverse, True))
        keep(x_ref, stage(held(x_ref), inverse, False))
        return held(x_ref)

    def times(a, b):
        return a[0] * b[0] - a[1] * b[1], a[0] * b[1] + a[1] * b[0]

    def conj_times(a, b):
        return a[0] * b[0] + a[1] * b[1], a[0] * b[1] - a[1] * b[0]

    spectrum = transform(times(held(probe_ref), held(patch_ref)), False)
    wave = transform(times(held(h_ref), spectrum), True)
    keep(wave_ref, wave)
    far = transform(times(held(wave_ref), held(patch_ref, 2)), False)
    modulus = jnp.maximum(jnp.sqrt(far[0] * far[0] + far[1] * far[1]), MOD_FLOOR)
    ratio = amp_ref[...] / modulus
    back = transform((far[0] - ratio * far[0], far[1] - ratio * far[1]), True)
    keep(wave_ref, conj_times(held(wave_ref), back))
    toward = transform(conj_times(held(patch_ref, 2), back), False)
    keep(x_ref, stage(conj_times(held(h_ref), toward), True, True))
    mine = pl.ds((me_ref[1] - col + 1024) & (C - 1), CLASS_IN_PATCH, stride=C)
    back = stage(held(x_ref, 0, mine), True, False)
    first_grad = conj_times(held(probe_ref, 0, mine), back)
    second_grad = held(wave_ref, 0, mine)
    alive = (count_ref[0] > 0).astype(F32)
    grads = jnp.concatenate([*first_grad, *second_grad], axis=0) * alive
    rows_ref[...] = jnp.zeros_like(rows_ref)
    rows_ref[pl.ds(row & 7, N), :] = grads.T
    first = lax.shift_right_logical(row, 3)
    for m in range(Z * TILES_PER_Z):
        k = m // Z
        o_ref[lax.rem(first + m, Z), k * TILE : (k + 1) * TILE] = rows_ref[
            m * TILE : (m + 1) * TILE
        ]


def gather_kernel(off_ref, me_ref, x_ref, o_ref, sum_ref):
    lane = lanes()
    sum_ref[...] = jnp.zeros_like(sum_ref)
    for z in range(Z):
        y_first, u_first = window(off_ref, me_ref, z)
        inside = between(lane, u_first, CLASS_IN_PATCH)
        for k in range(TILES_PER_Z):
            piece = x_ref[z, k * TILE : (k + 1) * TILE]
            for p in range(PLANES):
                moved = jnp.where(inside, rolled(piece, u_first - 32 * p), 0.0)
                sum_ref[p, y_first + k] += moved
    masks, low = [spread_masks(CLASS_IN_STRIP * j) for j in range(C)], upper_half()
    for y in range(Y):
        lines = [two_shifts(sum_ref[p, y], 32 * p, low) for p in range(PLANES)]
        for j in range(C):
            piece = jnp.zeros((TILE, LANES), F32)
            for p in range(PLANES):
                piece = jnp.where(masks[j][p], lines[p], piece)
            o_ref[y * C + j] = folded(piece)


def merge_kernel(me_ref, x_ref, order_ref, o_ref):
    lane, low = lanes(), upper_half()
    shift = CLASS_IN_STRIP * me_ref[1]
    sums = []
    for j in range(C):
        total = x_ref[j]
        for y in range(1, Y):
            total = total + x_ref[y * C + j]
        sums.append(unfolded(total))
    planes = []
    for p in range(PLANES):
        line = jnp.zeros((TILE, LANES), F32)
        for j in range(C):
            start = 16 * j - shift - 32 * p
            moved = jnp.where(low, rolled(sums[j], start), rolled(sums[j], start - 16))
            line = jnp.where(between(lane, 16 * j, CLASS_IN_STRIP), moved, line)
        planes.append(line)
    ordered = jnp.concatenate(planes, axis=0)
    tile = jnp.dot(
        ordered, order_ref[...], precision=lax.Precision.HIGHEST, preferred_element_type=F32
    )
    o_ref[...] = tile.reshape(2, 2, TILE, C * CLASS_IN_STRIP)


IN_VMEM = pl.BlockSpec(memory_space=pltpu.VMEM)
IN_SMEM = pl.BlockSpec(memory_space=pltpu.SMEM)


def call(kernel, out_shape, scalars, arrays, scratch=(), limit=8):
    return pl.pallas_call(
        kernel,
        out_shape=jax.ShapeDtypeStruct(out_shape, F32),
        in_specs=[IN_SMEM] * len(scalars) + [IN_VMEM] * len(arrays),
        out_specs=IN_VMEM,
        scratch_shapes=[pltpu.VMEM(shape, F32) for shape in scratch],
        compiler_params=pltpu.CompilerParams(vmem_limit_bytes=limit * 1024 * 1024),
    )(*scalars, *arrays)


def per_device(object_layers, probe_field, prop_phase, amplitude, offsets, counts):
    order = class_order()
    strip_shape = (PLANES, Y + 1, TILE, LANES)
    fold_shape = (Y * C, TILE // 2, LANES)
    piece_shape = (Z, TILES_PER_Z * TILE, LANES)
    rows_shape = (Z * TILES_PER_Z * TILE + TILE, LANES)
    halves = (2, N, LANES)
    me = jnp.stack(
        [lax.axis_index("pos_1"), lax.axis_index("col_0") * CORES + lax.axis_index("col_1")]
    ).astype(jnp.int32)
    line_offsets = exchange(jnp.broadcast_to(offsets[None], (Z, 1, 2)), "pos_1")
    split = call(split_kernel, fold_shape, (me,), (object_layers, jnp.asarray(order)))
    columns = exchange(split, ("pos_0", "col_0", "col_1"))
    chosen = call(select_kernel, piece_shape, (line_offsets, me), (columns,), (strip_shape,))
    rows = exchange(chosen, "pos_1")
    packed = call(
        pack_kernel,
        (CHIPS, N, N),
        (offsets,),
        (rows, prop_phase.T, amplitude[0].T, probe_field),
        (rows_shape,),
    )
    gathered = exchange(packed, "col_0")
    other = lax.ppermute(gathered, "col_1", [(0, 1), (1, 0)])
    grads = call(
        main_kernel,
        piece_shape,
        (offsets, counts, me),
        (gathered, other, jnp.asarray(dft_tables())),
        ((4, *halves), (2, *halves), (N, N), (2, N, N), (2, *halves), (2, *halves), (2, *halves), rows_shape),
        limit=24,
    )
    returned = exchange(grads, "pos_1")
    summed = call(gather_kernel, fold_shape, (line_offsets, me), (returned,), (strip_shape,))
    tiles = exchange(summed, ("pos_0", "col_0", "col_1"))
    return call(
        merge_kernel, (2, 2, TILE, C * CLASS_IN_STRIP), (me,), (tiles, jnp.asarray(order.T))
    )


COL = ("col_0", "col_1")


def solution(mesh):
    finer = Mesh(mesh.devices.reshape(Y, Z, CHIPS, CORES), POS + COL)
    return jax.shard_map(
        per_device,
        mesh=finer,
        in_specs=(
            P(None, None, POS, COL),
            P(None, COL, None),
            P(None, COL),
            P(POS, None, COL),
            P(POS, None),
            P(POS),
        ),
        out_specs=P(None, None, POS, COL),
        check_vma=False,
    )
```

time: 156 us -> 132 us (0.85)
  waiting for transfers between devices: 28.6 us -> 8.86 us
  blocking collectives: 68.5 us -> 84.7 us
  starting transfers between devices: 31.4 us -> 20.8 us
  Pallas kernels: 20.5 us -> 13.1 us
  other arithmetic: 1.87 us -> 0.08 us
    all_to_all x3 -> x1, waiting for transfers between devices: 28.6 us -> 7.24 us  [exchange(): return lax.all_to_all(x, axes, 0, 0, tiled=True)]
    all_to_all x3 -> x5, blocking collectives: 68.5 us -> 84.7 us  [exchange(): return lax.all_to_all(x, axes, 0, 0, tiled=True)]
    all_to_all x3 -> x1, starting transfers between devices: 31.4 us -> 15.7 us  [exchange(): return lax.all_to_all(x, axes, 0, 0, tiled=True)]
    pallas_call x6, Pallas kernels: 20.5 us -> 13.1 us  [call(): pl.pallas_call(kernel, out_shape=jax.ShapeDtypeStruct(out_shape, F32), in...]
    ppermute x0 -> x1, starting transfers between devices: none -> 5.13 us  [per_device(): other = lax.ppermute(gathered, 'col_1', [(0, 1), (1, 0)])]
    ppermute x0 -> x1, waiting for transfers between devices: none -> 1.62 us  [per_device(): other = lax.ppermute(gathered, 'col_1', [(0, 1), (1, 0)])]
  transfers between devices with their start and end apart: 3 -> 2, of which waited for: 3 -> 2; matrix products, arithmetic and copies ran while one was open for 2% -> 0% of each run, Pallas kernels for 1% -> 1%
where the time goes in v2:
time: 132 us; the launch traced here: 131 us
  blocking collectives  84.7 us (64%)
  starting transfers between devices  20.8 us (16%)
  Pallas kernels  13.1 us (10%)
  waiting for transfers between devices  8.86 us (7%)
  local copies, waits for them, and re-layouts  2.66 us (2%)
    all_to_all x5, blocking collectives, exchange(): return lax.all_to_all(x, axes, 0, 0, tiled=True)  84.7 us
    all_to_all x1, starting transfers between devices, exchange(): return lax.all_to_all(x, axes, 0, 0, tiled=True)  15.7 us
    pallas_call x6, Pallas kernels, call(): pl.pallas_call(kernel, out_shape=jax.ShapeDtypeStruct(out_shape, F32), in...  13.1 us
    all_to_all x1, waiting for transfers between devices, exchange(): return lax.all_to_all(x, axes, 0, 0, tiled=True)  7.24 us
    ppermute x1, starting transfers between devices, per_device(): other = lax.ppermute(gathered, 'col_1', [(0, 1), (1, 0)])  5.13 us
  transfers between devices with their start and end apart: 2, of which 2 were waited for; matrix products, arithmetic and copies ran while one was open for 0% of the time, Pallas kernels for 1%

profile of v2, /device:TPU:1, one launch (start us, length us, event | category | flops | bytes accessed | tf_op | source)
XLA Modules:
  0.0 131.0 jit_solution(10481289630467405801)
XLA Ops:
  0.0 1.3 broadcast_in_dim.9
  1.3 15.7 %all-to-all-start = ((s32[12,1,2]{2,1,0:T(1,128)}), s32[12,1,2]{2,1,0:T(1,128)S(1)}, u32[]{:S(2)}, u32[]{:S(2)}) async-start(s32[12,1,2]{2,1,0:T(1,128)} %broadcast_in_dim.9), calls=%async_computation | async-start | bytes 12288 | tf_op jit(solution)/shard_map/all_to_all | solution.py:27
  17.0 0.1 pad_add_fusion.me_ref
  17.1 0.7 copy-done.6
  17.8 0.8 shard_map.91
  18.6 7.2 %all-to-all-done.off_ref = s32[12,1,2]{2,1,0:T(1,128)S(1)} async-done(((s32[12,1,2]{2,1,0:T(1,128)}), s32[12,1,2]{2,1,0:T(1,128)S(1)}, u32[]{:S(2)}, u32[]{:S(2)}) %all-to-all-start) | async-done | bytes 128 | tf_op jit(solution)/shard_map/all_to_all | solution.py:27
  25.8 23.1 %all_to_all.30.x_ref = f32[64,4,128]{2,1,0:T(4,128)S(1)} all-to-all(f32[64,4,128]{2,1,0:T(4,128)S(1)} %shard_map.91), channel_id=1, replica_groups=mesh['pos_0'=8,'pos_1'=12,'col_0'=4,'col_1'=2] {'pos_0','col_0','col_1'}, dimensions={0} | all-to-all | bytes 262144 | tf_op jit(solution)/shard_map/all_to_all | solution.py:27
  48.9 1.0 shard_map.92
  49.9 0.0 copy-start.1
  50.0 0.0 copy-start.4
  50.0 0.0 copy-start.5
  50.0 14.2 %all_to_all.31.x_ref = f32[12,24,128]{2,1,0:T(8,128)S(1)} all-to-all(f32[12,24,128]{2,1,0:T(8,128)S(1)} %shard_map.92), channel_id=1, replica_groups=mesh['pos_0'=8,'pos_1'=12,'col_0'=4,'col_1'=2] {'pos_1'}, dimensions={0} | all-to-all | bytes 294912 | tf_op jit(solution)/shard_map/all_to_all | solution.py:27
  64.2 0.6 copy-done.7
  64.8 0.7 shard_map.93
  65.5 0.0 copy-start
  65.6 15.4 %all_to_all.32.g_ref = f32[4,256,256]{2,1,0:T(8,128)S(1)} all-to-all(f32[4,256,256]{2,1,0:T(8,128)S(1)} %shard_map.93), channel_id=1, replica_groups=mesh['pos_0'=8,'pos_1'=12,'col_0'=4,'col_1'=2] {'col_0'}, dimensions={0} | all-to-all | bytes 2097152 | tf_op jit(solution)/shard_map/all_to_all | solution.py:27
  80.9 5.1 %collective-permute-start = (f32[4,256,256]{2,1,0:T(8,128)S(1)}, f32[4,256,256]{2,1,0:T(8,128)S(1)}, u32[]{:S(2)}, u32[]{:S(2)}) collective-permute-start(f32[4,256,256]{2,1,0:T(8,128)S(1)} %all_to_all.32.g_ref), channel_id=1, source_target_pairs={{0,1},{1,0},{2,3},{3,2},{4,5},{5,4},{6,7},{7,6},{8,9},{9,8},{10,11... | collective-permute-start | bytes 3145736 | tf_op jit(solution)/shard_map/ppermute | solution.py:346
  86.7 1.6 %collective-permute-done.other_ref = f32[4,256,256]{2,1,0:T(8,128)S(1)} collective-permute-done((f32[4,256,256]{2,1,0:T(8,128)S(1)}, f32[4,256,256]{2,1,0:T(8,128)S(1)}, u32[]{:S(2)}, u32[]{:S(2)}) %collective-permute-start) | collective-permute-done | bytes 1048608 | tf_op jit(solution)/shard_map/ppermute | solution.py:346
  88.3 8.1 %shard_map.94 = f32[12,24,128]{2,1,0:T(8,128)S(1)} custom-call(s32[1,2]{1,0:T(1,128)S(1)} %copy-done.7, s32[1]{0:T(128)S(6)} %copy.10.count_ref, s32[2]{0:T(128)S(1)} %pad_add_fusion.me_ref, f32[4,256,256]{2,1,0:T(8,128)S(1)} %all_to_all.32.g_ref, f32[4,256,256]{2,1,0:T(8,128)S(1)} %collective-permute-done.other_ref, bf16[6,256,256]{2,1,0:T(8,128)(2,1)S(1)} %copy-done), custom_call_target="tpu_custom_call" | custom-call | tf_op jit(solution)/shard_map/pallas_call | solution.py:313
  96.5 14.9 %all_to_all.33.x_ref = f32[12,24,128]{2,1,0:T(8,128)S(1)} all-to-all(f32[12,24,128]{2,1,0:T(8,128)S(1)} %shard_map.94), channel_id=1, replica_groups=mesh['pos_0'=8,'pos_1'=12,'col_0'=4,'col_1'=2] {'pos_1'}, dimensions={0} | all-to-all | bytes 294912 | tf_op jit(solution)/shard_map/all_to_all | solution.py:27
  111.4 1.0 shard_map.95
  112.4 0.0 copy-start.2
  112.4 17.1 %all_to_all.34.x_ref = f32[64,4,128]{2,1,0:T(4,128)S(1)} all-to-all(f32[64,4,128]{2,1,0:T(4,128)S(1)} %shard_map.95), channel_id=1, replica_groups=mesh['pos_0'=8,'pos_1'=12,'col_0'=4,'col_1'=2] {'pos_0','col_0','col_1'}, dimensions={0} | all-to-all | bytes 262144 | tf_op jit(solution)/shard_map/all_to_all | solution.py:27
  129.6 1.4 %shard_map.96 = f32[2,2,8,96]{3,2,1,0:T(8,128)} custom-call(s32[2]{0:T(128)S(1)} %pad_add_fusion.me_ref, f32[64,4,128]{2,1,0:T(4,128)S(1)} %all_to_all.34.x_ref, f32[128,96]{1,0:T(8,128)S(1)} %copy-done.2), custom_call_target="tpu_custom_call" | custom-call | tf_op jit(solution)/shard_map/pallas_call | solution.py:313
  (9 shorter events, 0.0 us)
Async XLA Ops:
  0.0 17.1 %copy-start.3 = (f32[96,128]{1,0:T(8,128)S(1)}, f32[96,128]{1,0:T(8,128)}, u32[]{:S(2)}) copy-start(f32[96,128]{1,0:T(8,128)} %constant.20.clone.order_ref) | copy-start | bytes 147460
  1.3 24.6 %all-to-all-start = ((s32[12,1,2]{2,1,0:T(1,128)}), s32[12,1,2]{2,1,0:T(1,128)S(1)}, u32[]{:S(2)}, u32[]{:S(2)}) async-start(s32[12,1,2]{2,1,0:T(1,128)} %broadcast_in_dim.9), calls=%async_computation | async-start | bytes 12288 | tf_op jit(solution)/shard_map/all_to_all | solution.py:27
  17.1 0.7 copy-start.6
  49.9 14.2 %copy-start.1 = (f32[2,32,256]{2,1,0:T(8,128)S(1)}, f32[2,32,256]{2,1,0:T(8,128)}, u32[]{:S(2)}) copy-start(f32[2,32,256]{2,1,0:T(8,128)} %probe_ref.1) | copy-start | bytes 196612
  50.0 14.2 %copy-start.4 = (f32[256,32]{0,1:T(8,128)S(1)}, f32[256,32]{0,1:T(8,128)}, u32[]{:S(2)}) copy-start(f32[256,32]{0,1:T(8,128)} %param.11) | copy-start | bytes 98308
  50.0 14.2 %copy-start.5 = (f32[1,256,32]{1,2,0:T(8,128)S(1)}, f32[1,256,32]{1,2,0:T(8,128)}, u32[]{:S(2)}) copy-start(f32[1,256,32]{1,2,0:T(8,128)} %param.12) | copy-start | bytes 98308
  64.2 0.7 copy-start.7
  65.5 22.8 %copy-start = (bf16[6,256,256]{2,1,0:T(8,128)(2,1)S(1)}, bf16[6,256,256]{2,1,0:T(8,128)(2,1)}, u32[]{:S(2)}) copy-start(bf16[6,256,256]{2,1,0:T(8,128)(2,1)} %constant.21.clone.tab_ref) | copy-start | bytes 2359300
  80.9 7.4 %collective-permute-start = (f32[4,256,256]{2,1,0:T(8,128)S(1)}, f32[4,256,256]{2,1,0:T(8,128)S(1)}, u32[]{:S(2)}, u32[]{:S(2)}) collective-permute-start(f32[4,256,256]{2,1,0:T(8,128)S(1)} %all_to_all.32.g_ref), channel_id=1, source_target_pairs={{0,1},{1,0},{2,3},{3,2},{4,5},{5,4},{6,7},{7,6},{8,9},{9,8},{10,11... | collective-permute-start | bytes 3145736 | tf_op jit(solution)/shard_map/ppermute | solution.py:346
  112.4 17.2 %copy-start.2 = (f32[128,96]{1,0:T(8,128)S(1)}, f32[128,96]{1,0:T(8,128)}, u32[]{:S(2)}) copy-start(f32[128,96]{1,0:T(8,128)} %constant.22.clone.order_ref) | copy-start | bytes 147460

commit v3 on v2

v3 whole, which is shorter than its diff:
```python
import math

import jax
import jax.numpy as jnp
import numpy as np
from jax import lax
from jax.experimental import pallas as pl
from jax.experimental.pallas import tpu as pltpu
from jax.sharding import Mesh
from jax.sharding import PartitionSpec as P

POS = ("pos_0", "pos_1")
MOD_FLOOR = 0.1

Y, Z, C = 8, 12, 8
CHIPS, CORES = 4, 2
N = 256
PLANES = 4
TILE = 8
CLASS_IN_STRIP = 12
CLASS_IN_PATCH = 32
TILES_PER_Z = 3
LANES = 128
CHUNK = 32
F32 = jnp.float32
SINE_SERIES = [(-1.0) ** k / math.factorial(2 * k + 1) for k in range(6)]
COSINE_SERIES = [(-1.0) ** k / math.factorial(2 * k) for k in range(7)]
BF16 = jnp.bfloat16


def exchange(x, axes):
    return lax.all_to_all(x, axes, 0, 0, tiled=True)


def class_order(shape, column_axis):
    column = lax.broadcasted_iota(jnp.int32, shape, column_axis)
    lane = lax.broadcasted_iota(jnp.int32, shape, 1 - column_axis)
    place = (column & (C - 1)) * 16 + lax.shift_right_logical(column, 3)
    return (place == lane).astype(F32)


def dft_tables():
    counter = np.arange(N)
    angle = (counter[:, None] * counter[None, :] % N) * (2.0 * np.pi / N)
    cosine, sine = np.cos(angle) / 16.0, np.sin(angle) / 16.0
    parts = []
    for table in (cosine, cosine + sine, cosine - sine):
        table = table.astype(np.float32)
        high = table.astype(jnp.bfloat16)
        low = (table - high.astype(np.float32)).astype(jnp.bfloat16)
        parts += [high, low]
    return np.stack(parts)


def lanes():
    return lax.broadcasted_iota(jnp.int32, (TILE, LANES), 1)


def between(lane, low, width):
    return (lane >= low) & (lane < low + width)


def rolled(x, shift):
    if isinstance(shift, int):
        shift = shift % LANES
        return pltpu.roll(x, shift, 1) if shift else x
    return pltpu.roll(x, (shift + 2 * LANES) & (LANES - 1), 1)


def spread_masks(shift):
    lane = lanes()
    row = lax.broadcasted_iota(jnp.int32, (TILE, LANES), 0)
    base = lane - jnp.where(row < 4, 0, 16) - shift + 4 * LANES
    return [((base - 32 * p) & (LANES - 1)) < CLASS_IN_STRIP for p in range(PLANES)]


def upper_half():
    return lax.broadcasted_iota(jnp.int32, (TILE, LANES), 0) < 4


def folded(piece):
    return (piece + pltpu.roll(piece, 4, 0))[:4]


def unfolded(piece):
    return jnp.concatenate([piece, piece], axis=0)


def two_shifts(x, shift, low):
    return jnp.where(low, rolled(x, shift), rolled(x, shift + 16))


def split_kernel(me_ref, own_ref, x_ref, o_ref):
    shift = CLASS_IN_STRIP * me_ref[1]
    tile = x_ref[...].reshape(PLANES * TILE, C * CLASS_IN_STRIP)
    order = class_order((C * CLASS_IN_STRIP, LANES), 0)
    ordered = jnp.dot(
        tile, order, precision=lax.Precision.HIGHEST, preferred_element_type=F32
    )
    lane = lanes()
    base = lane - shift + 4 * LANES
    row, col = own_ref[0, 0].astype(F32), own_ref[0, 1].astype(F32)
    corner = jnp.where((base & (LANES - 1)) == CLASS_IN_STRIP, row, 0.0)
    corner = jnp.where((base & (LANES - 1)) == CLASS_IN_STRIP + 1, col, corner)
    for j in range(C):
        piece = corner
        for p in range(PLANES):
            moved = rolled(ordered[p * TILE : (p + 1) * TILE], shift + 32 * p - 16 * j)
            piece = jnp.where(((base - 32 * p) & (LANES - 1)) < CLASS_IN_STRIP, moved, piece)
        o_ref[j * TILE : (j + 1) * TILE] = piece


def widen_kernel(own_ref, x_ref, o_ref):
    lane = lanes()
    row, col = own_ref[0, 0].astype(F32), own_ref[0, 1].astype(F32)
    for p in range(PLANES):
        line = x_ref[0:TILE]
        for j in range(1, C):
            inside = ((lane - CLASS_IN_STRIP * j - 32 * p + 2 * LANES) & (LANES - 1)) < CLASS_IN_STRIP
            line = jnp.where(inside, x_ref[j * TILE : (j + 1) * TILE], line)
        line = rolled(line, -32 * p)
        line = jnp.where(lane == C * CLASS_IN_STRIP, row, line)
        line = jnp.where(lane == C * CLASS_IN_STRIP + 1, col, line)
        for z in range(Z):
            o_ref[z, p * TILE : (p + 1) * TILE] = line


def window(off_ref, me_ref, z):
    row, col = off_ref[z, 0], off_ref[z, 1]
    z_me, c_me = me_ref[0], me_ref[1]
    first = lax.shift_right_logical(row, 3)
    ahead = lax.rem(z_me - first + 6 * Z, Z)
    y_first = lax.div(first + ahead - z_me, Z)
    u_first = lax.shift_right_logical(col - c_me + 7, 3)
    return y_first, u_first


def select_kernel(off_ref, me_ref, x_ref, o_ref, strip_ref):
    lane = lax.broadcasted_iota(jnp.int32, (CLASS_IN_PATCH, LANES), 1)
    for p in range(PLANES):
        for z in range(Z):
            strip_ref[p, pl.ds(z, Y, stride=Z), :] = x_ref[z, p * TILE : (p + 1) * TILE]
    for y in range(Y):
        n_first = lax.shift_right_logical(off_ref[y, 0] - me_ref[2] + 7, 3)
        u_first = lax.shift_right_logical(off_ref[y, 1] - me_ref[1] + 7, 3)
        rows = pl.ds(n_first, CLASS_IN_PATCH)
        piece = rolled(strip_ref[0, rows, :], LANES - u_first)
        for p in range(1, PLANES):
            moved = rolled(strip_ref[p, rows, :], 32 * p - u_first)
            piece = jnp.where(lane >= 32 * p, moved, piece)
        o_ref[y] = piece


def pack_kernel(own_ref, x_ref, phase_ref, amp_ref, probe_ref, o_ref, rows_ref):
    row = own_ref[0, 0]
    for s in range(Y):
        rows_ref[pl.ds(s, CLASS_IN_PATCH, stride=Y), :] = x_ref[(row + s) & (Y - 1)]
    patch = rows_ref[...].T
    for copy in range(CHIPS):
        o_ref[copy, 0:128] = patch
        o_ref[copy, 128:160] = phase_ref[...]
        o_ref[copy, 160:192] = amp_ref[...]
        o_ref[copy, 192:224] = probe_ref[0]
        o_ref[copy, 224:256] = probe_ref[1]


def two_terms(x):
    high = x.astype(BF16)
    return high, (x - high.astype(F32)).astype(BF16)


def product(first, second):
    return jnp.dot(
        jnp.concatenate([first[0], first[0], first[1]], axis=1),
        jnp.concatenate([second[0], second[1], second[0]], axis=0),
        preferred_element_type=F32,
    )


def cosine_and_sine(angle):
    half = 0.5 * angle
    square = half * half
    sine = jnp.full_like(square, SINE_SERIES[-1])
    for coefficient in SINE_SERIES[-2::-1]:
        sine = sine * square + coefficient
    cosine = jnp.full_like(square, COSINE_SERIES[-1])
    for coefficient in COSINE_SERIES[-2::-1]:
        cosine = cosine * square + coefficient
    sine = sine * half
    twice = sine + sine
    return 1.0 - twice * sine, twice * cosine


def store(ref, at, value):
    ref[at, 0] = value[:, :LANES]
    ref[at, 1] = value[:, LANES:]


def load(ref, at, rows=slice(None)):
    return jnp.concatenate([ref[at, 0, rows, :], ref[at, 1, rows, :]], axis=1)


def main_kernel(
    own_ref, count_ref, me_ref, g_ref, other_ref, tab_ref, o_ref,
    patch_ref, h_ref, amp_ref, raw_ref, probe_ref, wave_ref, x_ref, rows_ref, op_ref,
):
    row, col = own_ref[0, 0], own_ref[0, 1]
    core = me_ref[1] & 1
    for source_ref, core_of in ((g_ref, core), (other_ref, 1 - core)):
        for chip in range(CHIPS):
            j = CORES * chip + core_of
            s = (j - col + 1024) & (C - 1)
            mine = pl.ds(pl.multiple_of(32 * j, 32), 32)
            amp_ref[mine, :] = source_ref[chip, 160:192, :]
            raw_ref[0, mine, :] = source_ref[chip, 192:224, :]
            raw_ref[1, mine, :] = source_ref[chip, 224:256, :]
            for half in range(2):
                part = slice(half * LANES, (half + 1) * LANES)
                for p in range(PLANES):
                    patch_ref[p, half, pl.ds(s, CLASS_IN_PATCH, stride=C), :] = source_ref[
                        chip, p * 32 : (p + 1) * 32, part
                    ]
    store(probe_ref, 0, raw_ref[0].T)
    store(probe_ref, 1, raw_ref[1].T)

    def table(k):
        return tab_ref[2 * k], tab_ref[2 * k + 1]

    def held(ref, at=0, rows=slice(None)):
        return load(ref, at, rows), load(ref, at + 1, rows)

    def keep(ref, pair):
        store(ref, 0, pair[0])
        store(ref, 1, pair[1])

    def keep_rows(ref, rows, pair):
        for at in range(2):
            ref[at, 0, rows] = pair[at][:, :LANES]
            ref[at, 1, rows] = pair[at][:, LANES:]

    def stage(inverse, left, rows=N):
        real_table, imag_table = (1, 2) if inverse else (2, 1)

        def times(at, k):
            data = (op_ref[at, :rows], op_ref[at + 1, :rows])
            return product(table(k), data) if left else product(data, table(k))

        common = times(0, 0)
        return common - times(4, real_table), common - times(2, imag_table)

    def prepare(rows, pair):
        real, imag = pair
        for at, part in ((0, real + imag), (2, real), (4, imag)):
            op_ref[at, rows], op_ref[at + 1, rows] = two_terms(part)

    def chunks(step):
        for start in range(0, N, CHUNK):
            step(slice(start, start + CHUNK))

    def propagator():
        for source_ref, core_of in ((g_ref, core), (other_ref, 1 - core)):
            for chip in range(CHIPS):
                rows = pl.ds(pl.multiple_of(32 * (CORES * chip + core_of), 32), 32)
                keep_rows(h_ref, rows, cosine_and_sine(source_ref[chip, 128:160, :]))

    def transform(inverse, meanwhile=None):
        keep(x_ref, stage(inverse, True))
        if meanwhile:
            meanwhile()
        chunks(lambda rows: prepare(rows, held(x_ref, 0, rows)))
        keep(x_ref, stage(inverse, False))

    def times(a, b):
        return a[0] * b[0] - a[1] * b[1], a[0] * b[1] + a[1] * b[0]

    def conj_times(a, b):
        return a[0] * b[0] + a[1] * b[1], a[0] * b[1] - a[1] * b[0]

    def enter(rows):
        prepare(rows, times(held(probe_ref, 0, rows), held(patch_ref, 0, rows)))

    def propagate(rows):
        prepare(rows, times(held(h_ref, 0, rows), held(x_ref, 0, rows)))

    def modulate(rows):
        wave = held(x_ref, 0, rows)
        keep_rows(wave_ref, rows, wave)
        prepare(rows, times(wave, held(patch_ref, 2, rows)))

    def correct(rows):
        real, imag = held(x_ref, 0, rows)
        modulus = jnp.maximum(jnp.sqrt(real * real + imag * imag), MOD_FLOOR)
        ratio = amp_ref[rows] / modulus
        prepare(rows, (real - ratio * real, imag - ratio * imag))

    def turn_back(rows):
        back = held(x_ref, 0, rows)
        keep_rows(wave_ref, rows, conj_times(held(wave_ref, 0, rows), back))
        prepare(rows, conj_times(held(patch_ref, 2, rows), back))

    def propagate_back(rows):
        prepare(rows, conj_times(held(h_ref, 0, rows), held(x_ref, 0, rows)))

    chunks(enter)
    transform(False, propagator)
    chunks(propagate)
    transform(True)
    chunks(modulate)
    transform(False)
    chunks(correct)
    transform(True)
    chunks(turn_back)
    transform(False)
    chunks(propagate_back)
    keep(x_ref, stage(True, True))
    mine = pl.ds((me_ref[1] - col + 1024) & (C - 1), CLASS_IN_PATCH, stride=C)
    prepare(slice(0, CLASS_IN_PATCH), held(x_ref, 0, mine))
    back = stage(True, False, CLASS_IN_PATCH)
    first_grad = conj_times(held(probe_ref, 0, mine), back)
    second_grad = held(wave_ref, 0, mine)
    alive = (count_ref[0] > 0).astype(F32)
    grads = jnp.concatenate([*first_grad, *second_grad], axis=0) * alive
    rows_ref[...] = jnp.zeros_like(rows_ref)
    rows_ref[pl.ds(row & 7, N), :] = grads.T
    first = lax.shift_right_logical(row, 3)
    for m in range(Z * TILES_PER_Z):
        k = m // Z
        o_ref[lax.rem(first + m, Z), k * TILE : (k + 1) * TILE] = rows_ref[
            m * TILE : (m + 1) * TILE
        ]


def gather_kernel(off_ref, me_ref, x_ref, o_ref, sum_ref):
    lane = lanes()
    sum_ref[...] = jnp.zeros_like(sum_ref)
    for z in range(Z):
        y_first, u_first = window(off_ref, me_ref, z)
        inside = between(lane, u_first, CLASS_IN_PATCH)
        for k in range(TILES_PER_Z):
            piece = x_ref[z, k * TILE : (k + 1) * TILE]
            for p in range(PLANES):
                moved = jnp.where(inside, rolled(piece, u_first - 32 * p), 0.0)
                sum_ref[p, y_first + k] += moved
    masks, low = [spread_masks(CLASS_IN_STRIP * j) for j in range(C)], upper_half()
    for y in range(Y):
        lines = [two_shifts(sum_ref[p, y], 32 * p, low) for p in range(PLANES)]
        for j in range(C):
            piece = jnp.zeros((TILE, LANES), F32)
            for p in range(PLANES):
                piece = jnp.where(masks[j][p], lines[p], piece)
            o_ref[y * C + j] = folded(piece)


def merge_kernel(me_ref, x_ref, o_ref):
    lane, low = lanes(), upper_half()
    shift = CLASS_IN_STRIP * me_ref[1]
    sums = []
    for j in range(C):
        total = x_ref[j]
        for y in range(1, Y):
            total = total + x_ref[y * C + j]
        sums.append(unfolded(total))
    planes = []
    for p in range(PLANES):
        line = jnp.zeros((TILE, LANES), F32)
        for j in range(C):
            start = 16 * j - shift - 32 * p
            moved = jnp.where(low, rolled(sums[j], start), rolled(sums[j], start - 16))
            line = jnp.where(between(lane, 16 * j, CLASS_IN_STRIP), moved, line)
        planes.append(line)
    ordered = jnp.concatenate(planes, axis=0)
    order = class_order((LANES, C * CLASS_IN_STRIP), 1)
    tile = jnp.dot(
        ordered, order, precision=lax.Precision.HIGHEST, preferred_element_type=F32
    )
    o_ref[...] = tile.reshape(2, 2, TILE, C * CLASS_IN_STRIP)


IN_VMEM = pl.BlockSpec(memory_space=pltpu.VMEM)
IN_SMEM = pl.BlockSpec(memory_space=pltpu.SMEM)


def call(kernel, out_shape, scalars, arrays, scratch=(), limit=8, extra=()):
    return pl.pallas_call(
        kernel,
        out_shape=jax.ShapeDtypeStruct(out_shape, F32),
        in_specs=[IN_SMEM] * len(scalars) + [IN_VMEM] * len(arrays),
        out_specs=IN_VMEM,
        scratch_shapes=[pltpu.VMEM(shape, F32) for shape in scratch] + list(extra),
        compiler_params=pltpu.CompilerParams(vmem_limit_bytes=limit * 1024 * 1024),
    )(*scalars, *arrays)


def per_device(object_layers, probe_field, prop_phase, amplitude, offsets, counts):
    strip_shape = (PLANES, Y + 1, TILE, LANES)
    fold_shape = (Y * C, TILE // 2, LANES)
    piece_shape = (Z, TILES_PER_Z * TILE, LANES)
    rows_shape = (Z * TILES_PER_Z * TILE + TILE, LANES)
    halves = (2, N, LANES)
    col_at = lax.axis_index("col_0") * CORES + lax.axis_index("col_1")
    me = jnp.stack([lax.axis_index("pos_1"), col_at, lax.axis_index("pos_0")]).astype(jnp.int32)
    split = call(split_kernel, (C * TILE, LANES), (me, offsets), (object_layers,))
    lines = exchange(split.reshape(C * Y, 1, LANES), COL + ("pos_0",)).reshape(C * Y, LANES)
    y_offsets = lines[:Y, CLASS_IN_STRIP : CLASS_IN_STRIP + 2].astype(jnp.int32)
    wide = call(widen_kernel, (Z, PLANES * TILE, LANES), (offsets,), (lines,))
    blocks = exchange(wide, "pos_1")
    width = C * CLASS_IN_STRIP
    z_offsets = blocks[:, 0, width : width + 2].astype(jnp.int32)
    chosen = call(
        select_kernel,
        (Y, CLASS_IN_PATCH, LANES),
        (y_offsets, me),
        (blocks,),
        ((PLANES, Y * Z, LANES),),
    )
    rows = exchange(chosen, "pos_0")
    packed = call(
        pack_kernel,
        (CHIPS, N, N),
        (offsets,),
        (rows, prop_phase.T, amplitude[0].T, probe_field),
        ((N, LANES),),
    )
    gathered = exchange(packed, "col_0")
    other = lax.ppermute(gathered, "col_1", [(0, 1), (1, 0)])
    grads = call(
        main_kernel,
        piece_shape,
        (offsets, counts, me),
        (gathered, other, jnp.asarray(dft_tables())),
        ((4, *halves), (2, *halves), (N, N), (2, N, N), (2, *halves), (2, *halves), (2, *halves), rows_shape),
        limit=24,
        extra=[pltpu.VMEM((6, N, N), BF16)],
    )
    returned = exchange(grads, "pos_1")
    summed = call(gather_kernel, fold_shape, (z_offsets, me), (returned,), (strip_shape,))
    tiles = exchange(summed, ("pos_0", "col_0", "col_1"))
    return call(
        merge_kernel, (2, 2, TILE, C * CLASS_IN_STRIP), (me,), (tiles,)
    )


COL = ("col_0", "col_1")


def solution(mesh):
    finer = Mesh(mesh.devices.reshape(Y, Z, CHIPS, CORES), POS + COL)
    return jax.shard_map(
        per_device,
        mesh=finer,
        in_specs=(
            P(None, None, POS, COL),
            P(None, COL, None),
            P(None, COL),
            P(POS, None, COL),
            P(POS, None),
            P(POS),
        ),
        out_specs=P(None, None, POS, COL),
        check_vma=False,
    )
```

time: 132 us -> 130 us (0.985)
  blocking collectives: 84.7 us -> 64.5 us
  waiting for transfers between devices: 8.86 us -> 24.9 us
  starting transfers between devices: 20.8 us -> 23.4 us
  local copies, waits for them, and re-layouts: 2.66 us -> 0.86 us
    all_to_all x5 -> x4, blocking collectives: 84.7 us -> 64.5 us  [exchange(): return lax.all_to_all(x, axes, 0, 0, tiled=True)]
    all_to_all x1 -> x2, waiting for transfers between devices: 7.24 us -> 23.3 us  [exchange(): return lax.all_to_all(x, axes, 0, 0, tiled=True)]
    ppermute x1, starting transfers between devices: 5.13 us -> 6.53 us  [per_device(): other = lax.ppermute(gathered, 'col_1', [(0, 1), (1, 0)])]
    pallas_call x6 -> x7, Pallas kernels: 13.1 us -> 14.3 us  [call(): pl.pallas_call(kernel, out_shape=jax.ShapeDtypeStruct(out_shape, F32), in...]
    all_to_all x1 -> x2, starting transfers between devices: 15.7 us -> 16.8 us  [exchange(): return lax.all_to_all(x, axes, 0, 0, tiled=True)]
  transfers between devices with their start and end apart: 2 -> 3, of which waited for: 2 -> 3; matrix products, arithmetic and copies ran while one was open for 0% -> 0% of each run, Pallas kernels for 1% -> 0%
where the time goes in v3:
time: 130 us; the launch traced here: 129 us
  blocking collectives  64.5 us (50%)
  waiting for transfers between devices  24.9 us (19%)
  starting transfers between devices  23.4 us (18%)
  Pallas kernels  14.3 us (11%)
    all_to_all x4, blocking collectives, exchange(): return lax.all_to_all(x, axes, 0, 0, tiled=True)  64.5 us
    all_to_all x2, waiting for transfers between devices, exchange(): return lax.all_to_all(x, axes, 0, 0, tiled=True)  23.3 us
    all_to_all x2, starting transfers between devices, exchange(): return lax.all_to_all(x, axes, 0, 0, tiled=True)  16.8 us
    pallas_call x7, Pallas kernels, call(): pl.pallas_call(kernel, out_shape=jax.ShapeDtypeStruct(out_shape, F32), in...  14.3 us
    ppermute x1, starting transfers between devices, per_device(): other = lax.ppermute(gathered, 'col_1', [(0, 1), (1, 0)])  6.53 us
  transfers between devices with their start and end apart: 3, of which 3 were waited for; matrix products, arithmetic and copies ran while one was open for 0% of the time, Pallas kernels for 0%

profile of v3, /device:TPU:1, one launch (start us, length us, event | category | flops | bytes accessed | tf_op | source)
XLA Modules:
  0.0 128.9 jit_solution(1594672802975041011)
XLA Ops:
  0.0 0.1 pad_add_fusion.me_ref
  0.1 0.6 copy-done.4
  0.7 0.8 shard_map.73
  1.5 23.1 %all_to_all.30 = f32[64,1,128]{2,1,0:T(1,128)S(1)} all-to-all(f32[64,1,128]{2,1,0:T(1,128)S(1)} %bitcast.14), channel_id=1, replica_groups=mesh['pos_0'=8,'pos_1'=12,'col_0'=4,'col_1'=2] {'col_0','col_1','pos_0'}, dimensions={0} | all-to-all | bytes 65536 | tf_op jit(solution)/shard_map/all_to_all | solution.py:32
  24.6 1.3 %shard_map.74 = f32[12,32,128]{2,1,0:T(8,128)} custom-call(s32[1,2]{1,0:T(1,128)S(1)} %copy-done.5, f32[64,128]{1,0:T(8,128)S(1)} %bitcast.12), custom_call_target="tpu_custom_call" | custom-call | tf_op jit(solution)/shard_map/pallas_call | solution.py:384
  25.9 12.5 %all-to-all-start.1 = ((f32[12,32,128]{2,1,0:T(8,128)}), f32[12,32,128]{2,1,0:T(8,128)S(1)}, u32[]{:S(2)}, u32[]{:S(2)}) async-start(f32[12,32,128]{2,1,0:T(8,128)} %shard_map.74), calls=%async_computation.1 | async-start | bytes 393216 | tf_op jit(solution)/shard_map/all_to_all | solution.py:32
  38.4 0.1 slice_convert_fusion.1.off_ref
  38.4 12.2 %all-to-all-done.1.x_ref = f32[12,32,128]{2,1,0:T(8,128)S(1)} async-done(((f32[12,32,128]{2,1,0:T(8,128)}), f32[12,32,128]{2,1,0:T(8,128)S(1)}, u32[]{:S(2)}, u32[]{:S(2)}) %all-to-all-start.1) | async-done | bytes 196640 | tf_op jit(solution)/shard_map/all_to_all | solution.py:32
  50.7 0.8 shard_map.75
  51.5 10.5 %all_to_all.31.x_ref = f32[8,32,128]{2,1,0:T(8,128)S(1)} all-to-all(f32[8,32,128]{2,1,0:T(8,128)S(1)} %shard_map.75), channel_id=1, replica_groups=mesh['pos_0'=8,'pos_1'=12,'col_0'=4,'col_1'=2] {'pos_0'}, dimensions={0} | all-to-all | bytes 262144 | tf_op jit(solution)/shard_map/all_to_all | solution.py:32
  62.0 0.7 shard_map.76
  62.7 0.0 copy-start
  62.7 14.0 %all_to_all.32.g_ref = f32[4,256,256]{2,1,0:T(8,128)S(1)} all-to-all(f32[4,256,256]{2,1,0:T(8,128)S(1)} %shard_map.76), channel_id=1, replica_groups=mesh['pos_0'=8,'pos_1'=12,'col_0'=4,'col_1'=2] {'col_0'}, dimensions={0} | all-to-all | bytes 2097152 | tf_op jit(solution)/shard_map/all_to_all | solution.py:32
  76.6 6.5 %collective-permute-start = (f32[4,256,256]{2,1,0:T(8,128)S(1)}, f32[4,256,256]{2,1,0:T(8,128)S(1)}, u32[]{:S(2)}, u32[]{:S(2)}) collective-permute-start(f32[4,256,256]{2,1,0:T(8,128)S(1)} %all_to_all.32.g_ref), channel_id=1, source_target_pairs={{0,1},{1,0},{2,3},{3,2},{4,5},{5,4},{6,7},{7,6},{8,9},{9,8},{10,11... | collective-permute-start | bytes 3145736 | tf_op jit(solution)/shard_map/ppermute | solution.py:425
  83.8 1.6 %collective-permute-done.other_ref = f32[4,256,256]{2,1,0:T(8,128)S(1)} collective-permute-done((f32[4,256,256]{2,1,0:T(8,128)S(1)}, f32[4,256,256]{2,1,0:T(8,128)S(1)}, u32[]{:S(2)}, u32[]{:S(2)}) %collective-permute-start) | collective-permute-done | bytes 1048608 | tf_op jit(solution)/shard_map/ppermute | solution.py:425
  85.5 8.2 %shard_map.77 = f32[12,24,128]{2,1,0:T(8,128)} custom-call(s32[1,2]{1,0:T(1,128)S(1)} %copy-done.5, s32[1]{0:T(128)S(6)} %copy.16.count_ref, s32[3]{0:T(128)S(1)} %pad_add_fusion.me_ref, f32[4,256,256]{2,1,0:T(8,128)S(1)} %all_to_all.32.g_ref, f32[4,256,256]{2,1,0:T(8,128)S(1)} %collective-permute-done.other_ref, bf16[6,256,256]{2,1,0:T(8,128)(2,1)S(1)} %copy-done), custom_call_target="tpu_custom_call" | custom-call | tf_op jit(solution)/shard_map/pallas_call | solution.py:384
  93.7 4.4 %all-to-all-start.4 = ((f32[12,24,128]{2,1,0:T(8,128)}), f32[12,24,128]{2,1,0:T(8,128)S(1)}, u32[]{:S(2)}, u32[]{:S(2)}) async-start(f32[12,24,128]{2,1,0:T(8,128)} %shard_map.77), calls=%async_computation.4 | async-start | bytes 294912 | tf_op jit(solution)/shard_map/all_to_all | solution.py:32
  98.0 0.1 slice_convert_fusion
  98.1 0.1 copy.14
  98.2 0.1 copy.15.off_ref
  98.3 11.1 %all-to-all-done.4.x_ref = f32[12,24,128]{2,1,0:T(8,128)S(1)} async-done(((f32[12,24,128]{2,1,0:T(8,128)}), f32[12,24,128]{2,1,0:T(8,128)S(1)}, u32[]{:S(2)}, u32[]{:S(2)}) %all-to-all-start.4) | async-done | bytes 147488 | tf_op jit(solution)/shard_map/all_to_all | solution.py:32
  109.4 1.0 shard_map.78
  110.4 17.0 %all_to_all.33.x_ref = f32[64,4,128]{2,1,0:T(4,128)S(1)} all-to-all(f32[64,4,128]{2,1,0:T(4,128)S(1)} %shard_map.78), channel_id=1, replica_groups=mesh['pos_0'=8,'pos_1'=12,'col_0'=4,'col_1'=2] {'pos_0','col_0','col_1'}, dimensions={0} | all-to-all | bytes 262144 | tf_op jit(solution)/shard_map/all_to_all | solution.py:32
  127.4 1.4 %shard_map.79 = f32[2,2,8,96]{3,2,1,0:T(8,128)} custom-call(s32[3]{0:T(128)S(1)} %pad_add_fusion.me_ref, f32[64,4,128]{2,1,0:T(4,128)S(1)} %all_to_all.33.x_ref), custom_call_target="tpu_custom_call" | custom-call | tf_op jit(solution)/shard_map/pallas_call | solution.py:384
  (10 shorter events, 0.0 us)
Async XLA Ops:
  0.0 0.7 copy-start.4
  0.0 0.7 copy-start.5
  25.9 24.8 %all-to-all-start.1 = ((f32[12,32,128]{2,1,0:T(8,128)}), f32[12,32,128]{2,1,0:T(8,128)S(1)}, u32[]{:S(2)}, u32[]{:S(2)}) async-start(f32[12,32,128]{2,1,0:T(8,128)} %shard_map.74), calls=%async_computation.1 | async-start | bytes 393216 | tf_op jit(solution)/shard_map/all_to_all | solution.py:32
  51.5 10.5 %copy-start.1 = (f32[2,32,256]{2,1,0:T(8,128)S(1)}, f32[2,32,256]{2,1,0:T(8,128)}, u32[]{:S(2)}) copy-start(f32[2,32,256]{2,1,0:T(8,128)} %probe_ref.1) | copy-start | bytes 196612
  51.5 10.5 %copy-start.2 = (f32[256,32]{0,1:T(8,128)S(1)}, f32[256,32]{0,1:T(8,128)}, u32[]{:S(2)}) copy-start(f32[256,32]{0,1:T(8,128)} %param.9) | copy-start | bytes 98308
  51.5 10.5 %copy-start.3 = (f32[1,256,32]{1,2,0:T(8,128)S(1)}, f32[1,256,32]{1,2,0:T(8,128)}, u32[]{:S(2)}) copy-start(f32[1,256,32]{1,2,0:T(8,128)} %param.10) | copy-start | bytes 98308
  62.7 22.8 %copy-start = (bf16[6,256,256]{2,1,0:T(8,128)(2,1)S(1)}, bf16[6,256,256]{2,1,0:T(8,128)(2,1)}, u32[]{:S(2)}) copy-start(bf16[6,256,256]{2,1,0:T(8,128)(2,1)} %constant.20.clone.tab_ref) | copy-start | bytes 2359300
  76.6 8.8 %collective-permute-start = (f32[4,256,256]{2,1,0:T(8,128)S(1)}, f32[4,256,256]{2,1,0:T(8,128)S(1)}, u32[]{:S(2)}, u32[]{:S(2)}) collective-permute-start(f32[4,256,256]{2,1,0:T(8,128)S(1)} %all_to_all.32.g_ref), channel_id=1, source_target_pairs={{0,1},{1,0},{2,3},{3,2},{4,5},{5,4},{6,7},{7,6},{8,9},{9,8},{10,11... | collective-permute-start | bytes 3145736 | tf_op jit(solution)/shard_map/ppermute | solution.py:425
  93.7 15.7 %all-to-all-start.4 = ((f32[12,24,128]{2,1,0:T(8,128)}), f32[12,24,128]{2,1,0:T(8,128)S(1)}, u32[]{:S(2)}, u32[]{:S(2)}) async-start(f32[12,24,128]{2,1,0:T(8,128)} %shard_map.77), calls=%async_computation.4 | async-start | bytes 294912 | tf_op jit(solution)/shard_map/all_to_all | solution.py:32

commit v4 on v3

--- a/solution.py
+++ b/solution.py
@@ -18,6 +18,8 @@
 PLANES = 4
 TILE = 8
 CLASS_IN_STRIP = 12
+STRIP = C * CLASS_IN_STRIP
+PIECE = 26
 CLASS_IN_PATCH = 32
 TILES_PER_Z = 3
 LANES = 128
@@ -110,19 +112,25 @@
         o_ref[j * TILE : (j + 1) * TILE] = piece
 
 
-def widen_kernel(own_ref, x_ref, o_ref):
+def widen_kernel(own_ref, x_ref, o_ref, off_ref):
     lane = lanes()
-    row, col = own_ref[0, 0].astype(F32), own_ref[0, 1].astype(F32)
+    planes = []
     for p in range(PLANES):
         line = x_ref[0:TILE]
         for j in range(1, C):
             inside = ((lane - CLASS_IN_STRIP * j - 32 * p + 2 * LANES) & (LANES - 1)) < CLASS_IN_STRIP
             line = jnp.where(inside, x_ref[j * TILE : (j + 1) * TILE], line)
-        line = rolled(line, -32 * p)
-        line = jnp.where(lane == C * CLASS_IN_STRIP, row, line)
-        line = jnp.where(lane == C * CLASS_IN_STRIP + 1, col, line)
-        for z in range(Z):
-            o_ref[z, p * TILE : (p + 1) * TILE] = line
+        planes.append(rolled(line, -32 * p))
+    packed = [
+        jnp.where(lane < STRIP, planes[q], rolled(planes[3], STRIP - 32 * q)) for q in range(3)
+    ]
+    row, col = own_ref[0, 0].astype(F32), own_ref[0, 1].astype(F32)
+    corner = jnp.where(lane[: PIECE - 3 * TILE] == 0, row, col)
+    for z in range(Z):
+        for q in range(3):
+            o_ref[z * PIECE + q * TILE : z * PIECE + (q + 1) * TILE] = packed[q]
+        o_ref[z * PIECE + 3 * TILE : (z + 1) * PIECE] = corner
+    off_ref[...] = x_ref[0:TILE].astype(jnp.int32)
 
 
 def window(off_ref, me_ref, z):
@@ -135,14 +143,21 @@
     return y_first, u_first
 
 
-def select_kernel(off_ref, me_ref, x_ref, o_ref, strip_ref):
+def select_kernel(off_ref, me_ref, x_ref, o_ref, z_off_ref, strip_ref):
+    lane = lanes()
+    for z in range(Z):
+        packed = [x_ref[z * PIECE + q * TILE : z * PIECE + (q + 1) * TILE] for q in range(3)]
+        last = rolled(packed[2], 64 - STRIP)
+        last = jnp.where(lane < 64, rolled(packed[1], 32 - STRIP), last)
+        last = jnp.where(lane < 32, rolled(packed[0], -STRIP), last)
+        for p, line in enumerate(packed + [last]):
+            strip_ref[p, pl.ds(z, Y, stride=Z), :] = line
+        z_off_ref[z : z + 1] = x_ref[z * PIECE + 3 * TILE : z * PIECE + 3 * TILE + 1].astype(jnp.int32)
     lane = lax.broadcasted_iota(jnp.int32, (CLASS_IN_PATCH, LANES), 1)
-    for p in range(PLANES):
-        for z in range(Z):
-            strip_ref[p, pl.ds(z, Y, stride=Z), :] = x_ref[z, p * TILE : (p + 1) * TILE]
     for y in range(Y):
-        n_first = lax.shift_right_logical(off_ref[y, 0] - me_ref[2] + 7, 3)
-        u_first = lax.shift_right_logical(off_ref[y, 1] - me_ref[1] + 7, 3)
+        row, col = off_ref[y, CLASS_IN_STRIP], off_ref[y, CLASS_IN_STRIP + 1]
+        n_first = lax.shift_right_logical(row - me_ref[2] + 7, 3)
+        u_first = lax.shift_right_logical(col - me_ref[1] + 7, 3)
         rows = pl.ds(n_first, CLASS_IN_PATCH)
         piece = rolled(strip_ref[0, rows, :], LANES - u_first)
         for p in range(1, PLANES):
@@ -381,11 +396,13 @@
 
 
 def call(kernel, out_shape, scalars, arrays, scratch=(), limit=8, extra=()):
+    single = isinstance(out_shape, tuple)
+    outs = [jax.ShapeDtypeStruct(*out) for out in ([(out_shape, F32)] if single else out_shape)]
     return pl.pallas_call(
         kernel,
-        out_shape=jax.ShapeDtypeStruct(out_shape, F32),
+        out_shape=outs[0] if single else outs,
         in_specs=[IN_SMEM] * len(scalars) + [IN_VMEM] * len(arrays),
-        out_specs=IN_VMEM,
+        out_specs=IN_VMEM if single else [IN_VMEM] * len(outs),
         scratch_shapes=[pltpu.VMEM(shape, F32) for shape in scratch] + list(extra),
         compiler_params=pltpu.CompilerParams(vmem_limit_bytes=limit * 1024 * 1024),
     )(*scalars, *arrays)
@@ -401,14 +418,13 @@
     me = jnp.stack([lax.axis_index("pos_1"), col_at, lax.axis_index("pos_0")]).astype(jnp.int32)
     split = call(split_kernel, (C * TILE, LANES), (me, offsets), (object_layers,))
     lines = exchange(split.reshape(C * Y, 1, LANES), COL + ("pos_0",)).reshape(C * Y, LANES)
-    y_offsets = lines[:Y, CLASS_IN_STRIP : CLASS_IN_STRIP + 2].astype(jnp.int32)
-    wide = call(widen_kernel, (Z, PLANES * TILE, LANES), (offsets,), (lines,))
-    blocks = exchange(wide, "pos_1")
-    width = C * CLASS_IN_STRIP
-    z_offsets = blocks[:, 0, width : width + 2].astype(jnp.int32)
-    chosen = call(
+    wide, y_offsets = call(
+        widen_kernel, [((Z * PIECE, LANES), F32), ((Y, LANES), jnp.int32)], (offsets,), (lines,)
+    )
+    blocks = exchange(wide.reshape(Z, 1, PIECE * LANES), "pos_1").reshape(Z * PIECE, LANES)
+    chosen, z_offsets = call(
         select_kernel,
-        (Y, CLASS_IN_PATCH, LANES),
+        [((Y, CLASS_IN_PATCH, LANES), F32), ((Z, LANES), jnp.int32)],
         (y_offsets, me),
         (blocks,),
         ((PLANES, Y * Z, LANES),),

time: 130 us -> 126 us (0.969)
  blocking collectives: 64.5 us -> 103 us
  waiting for transfers between devices: 24.9 us -> 1.62 us
  starting transfers between devices: 23.4 us -> 6.52 us
    all_to_all x4 -> x6, blocking collectives: 64.5 us -> 103 us  [exchange(): return lax.all_to_all(x, axes, 0, 0, tiled=True)]
    all_to_all x2 -> x0, waiting for transfers between devices: 23.3 us -> none  [exchange(): return lax.all_to_all(x, axes, 0, 0, tiled=True)]
    all_to_all x2 -> x0, starting transfers between devices: 16.8 us -> none  [exchange(): return lax.all_to_all(x, axes, 0, 0, tiled=True)]
  transfers between devices with their start and end apart: 3 -> 1, of which waited for: 3 -> 1; matrix products, arithmetic and copies ran while one was open for 0% -> 0% of each run, Pallas kernels for 0% -> 0%
where the time goes in v4:
time: 126 us
  blocking collectives  103 us (82%)
  Pallas kernels  13.1 us (10%)
  starting transfers between devices  6.52 us (5%)
  waiting for transfers between devices  1.62 us (1%)
    all_to_all x6, blocking collectives, exchange(): return lax.all_to_all(x, axes, 0, 0, tiled=True)  103 us
    pallas_call x7, Pallas kernels, call(): pl.pallas_call(kernel, out_shape=outs[0] if single else outs, in_specs=[I...  13.1 us
    ppermute x1, starting transfers between devices, per_device(): other = lax.ppermute(gathered, 'col_1', [(0, 1), (1, 0)])  6.52 us
  transfers between devices with their start and end apart: 1, of which 1 were waited for; matrix products, arithmetic and copies ran while one was open for 0% of the time, Pallas kernels for 0%

profile of v4, /device:TPU:1, one launch (start us, length us, event | category | flops | bytes accessed | tf_op | source)
XLA Modules:
  0.0 126.0 jit_solution(12100700322125538349)
XLA Ops:
  0.0 0.1 pad_add_fusion.me_ref
  0.1 0.6 copy-done.4
  0.7 0.0 copy-done.5
  0.7 0.8 shard_map.73
  1.5 23.1 %all_to_all.30 = f32[64,1,128]{2,1,0:T(1,128)S(1)} all-to-all(f32[64,1,128]{2,1,0:T(1,128)S(1)} %bitcast.16), channel_id=1, replica_groups=mesh['pos_0'=8,'pos_1'=12,'col_0'=4,'col_1'=2] {'col_0','col_1','pos_0'}, dimensions={0} | all-to-all | bytes 65536 | tf_op jit(solution)/shard_map/all_to_all | solution.py:34
  24.6 0.7 shard_map.74
  25.3 23.6 %all_to_all.31 = f32[12,1,3328]{2,1,0:T(1,128)S(1)} all-to-all(f32[12,1,3328]{2,1,0:T(1,128)S(1)} %bitcast.14), channel_id=1, replica_groups=mesh['pos_0'=8,'pos_1'=12,'col_0'=4,'col_1'=2] {'pos_1'}, dimensions={0} | all-to-all | bytes 319488 | tf_op jit(solution)/shard_map/all_to_all | solution.py:34
  48.9 0.9 shard_map.75
  49.8 0.0 copy-start.1
  49.8 0.0 copy-start.2
  49.8 0.0 copy-start.3
  49.8 10.5 %all_to_all.32.x_ref = f32[8,32,128]{2,1,0:T(8,128)S(1)} all-to-all(f32[8,32,128]{2,1,0:T(8,128)S(1)} %get-tuple-element.12), channel_id=1, replica_groups=mesh['pos_0'=8,'pos_1'=12,'col_0'=4,'col_1'=2] {'pos_0'}, dimensions={0} | all-to-all | bytes 262144 | tf_op jit(solution)/shard_map/all_to_all | solution.py:34
  60.3 0.0 copy-done.1
  60.3 0.0 copy-done.2
  60.3 0.7 shard_map.76
  60.9 0.0 copy-start
  61.0 14.0 %all_to_all.33.g_ref = f32[4,256,256]{2,1,0:T(8,128)S(1)} all-to-all(f32[4,256,256]{2,1,0:T(8,128)S(1)} %shard_map.76), channel_id=1, replica_groups=mesh['pos_0'=8,'pos_1'=12,'col_0'=4,'col_1'=2] {'col_0'}, dimensions={0} | all-to-all | bytes 2097152 | tf_op jit(solution)/shard_map/all_to_all | solution.py:34
  74.9 6.5 %collective-permute-start = (f32[4,256,256]{2,1,0:T(8,128)S(1)}, f32[4,256,256]{2,1,0:T(8,128)S(1)}, u32[]{:S(2)}, u32[]{:S(2)}) collective-permute-start(f32[4,256,256]{2,1,0:T(8,128)S(1)} %all_to_all.33.g_ref), channel_id=1, source_target_pairs={{0,1},{1,0},{2,3},{3,2},{4,5},{5,4},{6,7},{7,6},{8,9},{9,8},{10,11... | collective-permute-start | bytes 3145736 | tf_op jit(solution)/shard_map/ppermute | solution.py:441
  82.1 1.6 %collective-permute-done.other_ref = f32[4,256,256]{2,1,0:T(8,128)S(1)} collective-permute-done((f32[4,256,256]{2,1,0:T(8,128)S(1)}, f32[4,256,256]{2,1,0:T(8,128)S(1)}, u32[]{:S(2)}, u32[]{:S(2)}) %collective-permute-start) | collective-permute-done | bytes 1048608 | tf_op jit(solution)/shard_map/ppermute | solution.py:441
  83.7 7.6 %shard_map.77 = f32[12,24,128]{2,1,0:T(8,128)S(1)} custom-call(s32[1,2]{1,0:T(1,128)S(1)} %copy-done.5, s32[1]{0:T(128)S(6)} %copy.10.count_ref, s32[3]{0:T(128)S(1)} %pad_add_fusion.me_ref, f32[4,256,256]{2,1,0:T(8,128)S(1)} %all_to_all.33.g_ref, f32[4,256,256]{2,1,0:T(8,128)S(1)} %collective-permute-done.other_ref, bf16[6,256,256]{2,1,0:T(8,128)(2,1)S(1)} %copy-done), custom_call_target="tpu_custom_call" | custom-call | tf_op jit(solution)/shard_map/pallas_call | solution.py:401
  91.3 15.2 %all_to_all.34.x_ref = f32[12,24,128]{2,1,0:T(8,128)S(1)} all-to-all(f32[12,24,128]{2,1,0:T(8,128)S(1)} %shard_map.77), channel_id=1, replica_groups=mesh['pos_0'=8,'pos_1'=12,'col_0'=4,'col_1'=2] {'pos_1'}, dimensions={0} | all-to-all | bytes 294912 | tf_op jit(solution)/shard_map/all_to_all | solution.py:34
  106.5 1.1 shard_map.78
  107.6 17.0 %all_to_all.35.x_ref = f32[64,4,128]{2,1,0:T(4,128)S(1)} all-to-all(f32[64,4,128]{2,1,0:T(4,128)S(1)} %shard_map.78), channel_id=1, replica_groups=mesh['pos_0'=8,'pos_1'=12,'col_0'=4,'col_1'=2] {'pos_0','col_0','col_1'}, dimensions={0} | all-to-all | bytes 262144 | tf_op jit(solution)/shard_map/all_to_all | solution.py:34
  124.6 1.4 %shard_map.79 = f32[2,2,8,96]{3,2,1,0:T(8,128)} custom-call(s32[3]{0:T(128)S(1)} %pad_add_fusion.me_ref, f32[64,4,128]{2,1,0:T(4,128)S(1)} %all_to_all.35.x_ref), custom_call_target="tpu_custom_call" | custom-call | tf_op jit(solution)/shard_map/pallas_call | solution.py:401
  (4 shorter events, 0.0 us)
Async XLA Ops:
  0.0 0.7 copy-start.4
  0.0 0.7 copy-start.5
  49.8 10.5 %copy-start.1 = (f32[2,32,256]{2,1,0:T(8,128)S(1)}, f32[2,32,256]{2,1,0:T(8,128)}, u32[]{:S(2)}) copy-start(f32[2,32,256]{2,1,0:T(8,128)} %probe_ref.1) | copy-start | bytes 196612
  49.8 10.5 %copy-start.2 = (f32[256,32]{0,1:T(8,128)S(1)}, f32[256,32]{0,1:T(8,128)}, u32[]{:S(2)}) copy-start(f32[256,32]{0,1:T(8,128)} %param.9) | copy-start | bytes 98308
  49.8 10.5 %copy-start.3 = (f32[1,256,32]{1,2,0:T(8,128)S(1)}, f32[1,256,32]{1,2,0:T(8,128)}, u32[]{:S(2)}) copy-start(f32[1,256,32]{1,2,0:T(8,128)} %param.10) | copy-start | bytes 98308
  60.9 22.8 %copy-start = (bf16[6,256,256]{2,1,0:T(8,128)(2,1)S(1)}, bf16[6,256,256]{2,1,0:T(8,128)(2,1)}, u32[]{:S(2)}) copy-start(bf16[6,256,256]{2,1,0:T(8,128)(2,1)} %constant.20.clone.tab_ref) | copy-start | bytes 2359300
  74.9 8.8 %collective-permute-start = (f32[4,256,256]{2,1,0:T(8,128)S(1)}, f32[4,256,256]{2,1,0:T(8,128)S(1)}, u32[]{:S(2)}, u32[]{:S(2)}) collective-permute-start(f32[4,256,256]{2,1,0:T(8,128)S(1)} %all_to_all.33.g_ref), channel_id=1, source_target_pairs={{0,1},{1,0},{2,3},{3,2},{4,5},{5,4},{6,7},{7,6},{8,9},{9,8},{10,11... | collective-permute-start | bytes 3145736 | tf_op jit(solution)/shard_map/ppermute | solution.py:441

commit v5 on v4

--- a/solution.py
+++ b/solution.py
@@ -46,7 +46,7 @@
     angle = (counter[:, None] * counter[None, :] % N) * (2.0 * np.pi / N)
     cosine, sine = np.cos(angle) / 16.0, np.sin(angle) / 16.0
     parts = []
-    for table in (cosine, cosine + sine, cosine - sine):
+    for table in (cosine, sine, -sine):
         table = table.astype(np.float32)
         high = table.astype(jnp.bfloat16)
         low = (table - high.astype(np.float32)).astype(jnp.bfloat16)
@@ -254,18 +254,35 @@
             ref[at, 1, rows] = pair[at][:, LANES:]
 
     def stage(inverse, left, rows=N):
-        real_table, imag_table = (1, 2) if inverse else (2, 1)
-
-        def times(at, k):
+        plus, minus = (2, 1) if inverse else (1, 2)
+
+        def terms(at, k):
             data = (op_ref[at, :rows], op_ref[at + 1, :rows])
-            return product(table(k), data) if left else product(data, table(k))
-
-        common = times(0, 0)
-        return common - times(4, real_table), common - times(2, imag_table)
+            return (table(k), data) if left else (data, table(k))
+
+        def total(*pairs):
+            return jnp.dot(
+                jnp.concatenate([part for f, s in pairs for part in (f[0], f[0], f[1])], axis=1),
+                jnp.concatenate([part for f, s in pairs for part in (s[0], s[1], s[0])], axis=0),
+                preferred_element_type=F32,
+            )
+
+        if left:
+            return total(terms(0, 0), terms(2, plus)), total(terms(2, 0), terms(0, minus))
+        real = [op_ref[t, :rows] for t in (0, 1)]
+        imag = [op_ref[2 + t, :rows] for t in (0, 1)]
+        upper = [jnp.concatenate([table(0)[t], table(minus)[t]], axis=1) for t in (0, 1)]
+        lower = [jnp.concatenate([table(plus)[t], table(0)[t]], axis=1) for t in (0, 1)]
+        both = jnp.dot(
+            jnp.concatenate([real[0], imag[0], real[0], imag[0], real[1], imag[1]], axis=1),
+            jnp.concatenate([upper[0], lower[0], upper[1], lower[1], upper[0], lower[0]], axis=0),
+            preferred_element_type=F32,
+        )
+        return both[:, :N], both[:, N:]
 
     def prepare(rows, pair):
         real, imag = pair
-        for at, part in ((0, real + imag), (2, real), (4, imag)):
+        for at, part in ((0, real), (2, imag)):
             op_ref[at, rows], op_ref[at + 1, rows] = two_terms(part)
 
     def chunks(step):
@@ -446,7 +463,7 @@
         (gathered, other, jnp.asarray(dft_tables())),
         ((4, *halves), (2, *halves), (N, N), (2, N, N), (2, *halves), (2, *halves), (2, *halves), rows_shape),
         limit=24,
-        extra=[pltpu.VMEM((6, N, N), BF16)],
+        extra=[pltpu.VMEM((4, N, N), BF16)],
     )
     returned = exchange(grads, "pos_1")
     summed = call(gather_kernel, fold_shape, (z_offsets, me), (returned,), (strip_shape,))

time: 126 us -> 126 us (level)
  no operation moved by 1% of the time
where the time goes in v5:
time: 126 us
  blocking collectives  103 us (82%)
  Pallas kernels  13.1 us (10%)
  starting transfers between devices  6.52 us (5%)
  waiting for transfers between devices  1.62 us (1%)
    all_to_all x6, blocking collectives, exchange(): return lax.all_to_all(x, axes, 0, 0, tiled=True)  103 us
    pallas_call x7, Pallas kernels, call(): pl.pallas_call(kernel, out_shape=outs[0] if single else outs, in_specs=[I...  13.1 us
    ppermute x1, starting transfers between devices, per_device(): other = lax.ppermute(gathered, 'col_1', [(0, 1), (1, 0)])  6.52 us
  transfers between devices with their start and end apart: 1, of which 1 were waited for; matrix products, arithmetic and copies ran while one was open for 0% of the time, Pallas kernels for 0%

profile of v5, /device:TPU:1, one launch (start us, length us, event | category | flops | bytes accessed | tf_op | source)
XLA Modules:
  0.0 126.0 jit_solution(7031359883325959956)
XLA Ops:
  0.0 0.1 pad_add_fusion.me_ref
  0.1 0.6 copy-done.4
  0.7 0.0 copy-done.5
  0.7 0.8 shard_map.73
  1.5 23.1 %all_to_all.30 = f32[64,1,128]{2,1,0:T(1,128)S(1)} all-to-all(f32[64,1,128]{2,1,0:T(1,128)S(1)} %bitcast.16), channel_id=1, replica_groups=mesh['pos_0'=8,'pos_1'=12,'col_0'=4,'col_1'=2] {'col_0','col_1','pos_0'}, dimensions={0} | all-to-all | bytes 65536 | tf_op jit(solution)/shard_map/all_to_all | solution.py:34
  24.6 0.7 shard_map.74
  25.3 23.6 %all_to_all.31 = f32[12,1,3328]{2,1,0:T(1,128)S(1)} all-to-all(f32[12,1,3328]{2,1,0:T(1,128)S(1)} %bitcast.14), channel_id=1, replica_groups=mesh['pos_0'=8,'pos_1'=12,'col_0'=4,'col_1'=2] {'pos_1'}, dimensions={0} | all-to-all | bytes 319488 | tf_op jit(solution)/shard_map/all_to_all | solution.py:34
  48.9 0.9 shard_map.75
  49.8 0.0 copy-start.1
  49.8 0.0 copy-start.2
  49.8 0.0 copy-start.3
  49.8 10.5 %all_to_all.32.x_ref = f32[8,32,128]{2,1,0:T(8,128)S(1)} all-to-all(f32[8,32,128]{2,1,0:T(8,128)S(1)} %get-tuple-element.12), channel_id=1, replica_groups=mesh['pos_0'=8,'pos_1'=12,'col_0'=4,'col_1'=2] {'pos_0'}, dimensions={0} | all-to-all | bytes 262144 | tf_op jit(solution)/shard_map/all_to_all | solution.py:34
  60.3 0.0 copy-done.1
  60.3 0.0 copy-done.3
  60.3 0.7 shard_map.76
  60.9 0.0 copy-start
  61.0 14.0 %all_to_all.33.g_ref = f32[4,256,256]{2,1,0:T(8,128)S(1)} all-to-all(f32[4,256,256]{2,1,0:T(8,128)S(1)} %shard_map.76), channel_id=1, replica_groups=mesh['pos_0'=8,'pos_1'=12,'col_0'=4,'col_1'=2] {'col_0'}, dimensions={0} | all-to-all | bytes 2097152 | tf_op jit(solution)/shard_map/all_to_all | solution.py:34
  74.9 6.5 %collective-permute-start = (f32[4,256,256]{2,1,0:T(8,128)S(1)}, f32[4,256,256]{2,1,0:T(8,128)S(1)}, u32[]{:S(2)}, u32[]{:S(2)}) collective-permute-start(f32[4,256,256]{2,1,0:T(8,128)S(1)} %all_to_all.33.g_ref), channel_id=1, source_target_pairs={{0,1},{1,0},{2,3},{3,2},{4,5},{5,4},{6,7},{7,6},{8,9},{9,8},{10,11... | collective-permute-start | bytes 3145736 | tf_op jit(solution)/shard_map/ppermute | solution.py:458
  82.1 1.6 %collective-permute-done.other_ref = f32[4,256,256]{2,1,0:T(8,128)S(1)} collective-permute-done((f32[4,256,256]{2,1,0:T(8,128)S(1)}, f32[4,256,256]{2,1,0:T(8,128)S(1)}, u32[]{:S(2)}, u32[]{:S(2)}) %collective-permute-start) | collective-permute-done | bytes 1048608 | tf_op jit(solution)/shard_map/ppermute | solution.py:458
  83.7 7.6 %shard_map.77 = f32[12,24,128]{2,1,0:T(8,128)S(1)} custom-call(s32[1,2]{1,0:T(1,128)S(1)} %copy-done.5, s32[1]{0:T(128)S(6)} %copy.10.count_ref, s32[3]{0:T(128)S(1)} %pad_add_fusion.me_ref, f32[4,256,256]{2,1,0:T(8,128)S(1)} %all_to_all.33.g_ref, f32[4,256,256]{2,1,0:T(8,128)S(1)} %collective-permute-done.other_ref, bf16[6,256,256]{2,1,0:T(8,128)(2,1)S(1)} %copy-done), custom_call_target="tpu_custom_call" | custom-call | tf_op jit(solution)/shard_map/pallas_call | solution.py:418
  91.3 15.2 %all_to_all.34.x_ref = f32[12,24,128]{2,1,0:T(8,128)S(1)} all-to-all(f32[12,24,128]{2,1,0:T(8,128)S(1)} %shard_map.77), channel_id=1, replica_groups=mesh['pos_0'=8,'pos_1'=12,'col_0'=4,'col_1'=2] {'pos_1'}, dimensions={0} | all-to-all | bytes 294912 | tf_op jit(solution)/shard_map/all_to_all | solution.py:34
  106.5 1.1 shard_map.78
  107.6 17.0 %all_to_all.35.x_ref = f32[64,4,128]{2,1,0:T(4,128)S(1)} all-to-all(f32[64,4,128]{2,1,0:T(4,128)S(1)} %shard_map.78), channel_id=1, replica_groups=mesh['pos_0'=8,'pos_1'=12,'col_0'=4,'col_1'=2] {'pos_0','col_0','col_1'}, dimensions={0} | all-to-all | bytes 262144 | tf_op jit(solution)/shard_map/all_to_all | solution.py:34
  124.6 1.4 %shard_map.79 = f32[2,2,8,96]{3,2,1,0:T(8,128)} custom-call(s32[3]{0:T(128)S(1)} %pad_add_fusion.me_ref, f32[64,4,128]{2,1,0:T(4,128)S(1)} %all_to_all.35.x_ref), custom_call_target="tpu_custom_call" | custom-call | tf_op jit(solution)/shard_map/pallas_call | solution.py:418
  (4 shorter events, 0.0 us)
Async XLA Ops:
  0.0 0.7 copy-start.4
  0.0 0.7 copy-start.5
  49.8 10.5 %copy-start.1 = (f32[2,32,256]{2,1,0:T(8,128)S(1)}, f32[2,32,256]{2,1,0:T(8,128)}, u32[]{:S(2)}) copy-start(f32[2,32,256]{2,1,0:T(8,128)} %probe_ref.1) | copy-start | bytes 196612
  49.8 10.5 %copy-start.2 = (f32[256,32]{0,1:T(8,128)S(1)}, f32[256,32]{0,1:T(8,128)}, u32[]{:S(2)}) copy-start(f32[256,32]{0,1:T(8,128)} %param.9) | copy-start | bytes 98308
  49.8 10.5 %copy-start.3 = (f32[1,256,32]{1,2,0:T(8,128)S(1)}, f32[1,256,32]{1,2,0:T(8,128)}, u32[]{:S(2)}) copy-start(f32[1,256,32]{1,2,0:T(8,128)} %param.10) | copy-start | bytes 98308
  60.9 22.8 %copy-start = (bf16[6,256,256]{2,1,0:T(8,128)(2,1)S(1)}, bf16[6,256,256]{2,1,0:T(8,128)(2,1)}, u32[]{:S(2)}) copy-start(bf16[6,256,256]{2,1,0:T(8,128)(2,1)} %constant.20.clone.tab_ref) | copy-start | bytes 2359300
  74.9 8.8 %collective-permute-start = (f32[4,256,256]{2,1,0:T(8,128)S(1)}, f32[4,256,256]{2,1,0:T(8,128)S(1)}, u32[]{:S(2)}, u32[]{:S(2)}) collective-permute-start(f32[4,256,256]{2,1,0:T(8,128)S(1)} %all_to_all.33.g_ref), channel_id=1, source_target_pairs={{0,1},{1,0},{2,3},{3,2},{4,5},{5,4},{6,7},{7,6},{8,9},{9,8},{10,11... | collective-permute-start | bytes 3145736 | tf_op jit(solution)/shard_map/ppermute | solution.py:458
